TPU v7x, 1024 devices: a whole 4x4x32 slice. The times are simulated.
1024 devices in a mesh: grp: 32 (over z), srv: 32 (over x, y, core).
Axes of the slice: x: 4, y: 4, z: 32, core: 2. Of those that a mesh axis runs over, the one named last changes fastest.
Arguments:
- queries: bfloat16 [8192, 8192], P('srv', 'grp'), may hold values from -8 to 8
- key_rows: bfloat16 [8192, 1024], P('srv'), may hold values from -8 to 8
- value_rows: bfloat16 [8192, 1024], P('srv'), may hold values from -6 to 6
- grad_output: bfloat16 [8192, 8192], P('srv', 'grp'), may hold values from -6 to 6
- doc_ids: int32 [8192], replicated, may hold values from 0 to 31, never falling along the last dimension, each value on 1 to 4352 neighbouring positions
Outputs:
- grad_query: bfloat16 [8192, 8192], P('srv', 'grp')
- grad_key: bfloat16 [8192, 1024], P('srv', 'grp')
- grad_value: bfloat16 [8192, 1024], P('srv', 'grp')
Inputs may be any that keep to these rules, and one draw needn't show every extreme that they name: `doc_ids`: document numbers never fall along the pack; each document has 1 to 4352 tokens, and one has exactly 4352.
All inputs are finite; a program needn't handle non-finite values.
Results may differ from a plain program's by a relative error of at most 0.0069.
Values may be sent and summed in bfloat16 or wider, within the bound.
A program may use at most 32 MiB of HBM per device.

v0:
```python
import jax
import jax.numpy as jnp
from jax import lax
from jax.sharding import PartitionSpec as P

HD = 128


big_negative = -1e30


def partner(block, axis, bit):
    count = lax.axis_size(axis)
    route = []
    for low in range(count):
        high = low | 1 << bit
        if high != low and high < count:
            route += [(low, high), (high, low)]
    return lax.ppermute(block, axis, route)


def score_block(query_heads, key_block, row_pos, row_doc, key_pos, key_doc):
    head_dim = key_block.shape[1]
    scores = jnp.einsum(
        "rhd,kd->hrk", query_heads, key_block, preferred_element_type=jnp.float32
    ) * head_dim ** (-0.5)
    allowed = (row_doc[:, None] == key_doc[None, :]) & (key_pos[None, :] <= row_pos[:, None])
    return (scores, allowed[None])


def stats_update(
    state_now, query_heads, grad_heads, key_block, value_block, row_pos, row_doc, key_pos, key_doc
):
    run_max, run_sum, run_acc = state_now
    scores, allowed = score_block(query_heads, key_block, row_pos, row_doc, key_pos, key_doc)
    grad_probs = jnp.einsum(
        "rhd,kd->hrk", grad_heads, value_block, preferred_element_type=jnp.float32
    )
    new_max = jnp.maximum(run_max, jnp.max(jnp.where(allowed, scores, big_negative), axis=2))
    factor = jnp.exp(run_max - new_max)
    weights = jnp.where(allowed, jnp.exp(scores - new_max[:, :, None]), 0.0)
    return (
        new_max,
        run_sum * factor + jnp.sum(weights, axis=2),
        run_acc * factor + jnp.sum(weights * grad_probs, axis=2),
    )


def gradient_terms(
    query_heads,
    grad_heads,
    key_block,
    value_block,
    log_norm,
    row_delta,
    row_pos,
    row_doc,
    key_pos,
    key_doc,
):
    scores, allowed = score_block(query_heads, key_block, row_pos, row_doc, key_pos, key_doc)
    weights = jnp.where(allowed, jnp.exp(scores - log_norm[:, :, None]), 0.0)
    grad_probs = jnp.einsum(
        "rhd,kd->hrk", grad_heads, value_block, preferred_element_type=jnp.float32
    )
    grad_scores = (weights * (grad_probs - row_delta[:, :, None])).astype(jnp.bfloat16)
    return (weights.astype(jnp.bfloat16), grad_scores)


def query_part(grad_scores, key_block):
    return jnp.einsum("hrk,kd->rhd", grad_scores, key_block, preferred_element_type=jnp.float32)


def key_value_part(weights_low, grad_scores, query_heads, grad_heads):
    head_dim = query_heads.shape[2]
    key_part = jnp.einsum(
        "hrk,rhd->kd", grad_scores, query_heads, preferred_element_type=jnp.float32
    ) * head_dim ** (-0.5)
    value_part = jnp.einsum(
        "hrk,rhd->kd", weights_low, grad_heads, preferred_element_type=jnp.float32
    )
    return jnp.concatenate([key_part, value_part], axis=1)


def on_device(queries, key_rows, value_rows, grad_output, doc_ids):
    row_count = queries.shape[0]
    head_dim = HD
    heads_here = queries.shape[1] // head_dim
    query_heads = queries.reshape(row_count, heads_here, head_dim)
    grad_heads = grad_output.reshape(row_count, heads_here, head_dim)
    kv_heads = key_rows.shape[1] // head_dim
    share = lax.axis_size("grp") // kv_heads
    kv_col = lax.axis_index("grp") // share * head_dim
    own_block = jnp.concatenate(
        [
            lax.dynamic_slice_in_dim(key_rows, kv_col, head_dim, 1),
            lax.dynamic_slice_in_dim(value_rows, kv_col, head_dim, 1),
        ],
        axis=1,
    )
    seq_index = lax.axis_index("srv")
    row_first = seq_index * row_count
    row_last = row_first + row_count - 1
    row_pos = row_first + jnp.arange(row_count, dtype=jnp.int32)
    row_doc = lax.dynamic_slice_in_dim(doc_ids, row_first, row_count)
    start_state = (
        jnp.full((heads_here, row_count), big_negative, jnp.float32),
        jnp.zeros((heads_here, row_count), jnp.float32),
        jnp.zeros((heads_here, row_count), jnp.float32),
    )
    zero_acc = jnp.zeros((row_count, heads_here, head_dim), jnp.float32)

    def reaches(first_key, span):
        last_doc = lax.dynamic_slice_in_dim(doc_ids, first_key + span - 1, 1)[0]
        return (first_key <= row_last) & (last_doc >= row_doc[0])

    def key_info(first_key, span):
        return (
            first_key + jnp.arange(span, dtype=jnp.int32),
            lax.dynamic_slice_in_dim(doc_ids, first_key, span),
        )

    def stats_on(state_now, kv_block, first_key):
        span = kv_block.shape[0]
        key_pos, key_doc = key_info(first_key, span)

        def stats_active(state_in):
            return stats_update(
                state_in,
                query_heads,
                grad_heads,
                kv_block[:, :head_dim],
                kv_block[:, head_dim:],
                row_pos,
                row_doc,
                key_pos,
                key_doc,
            )

        def stats_resting(state_in):
            return state_in

        return lax.cond(reaches(first_key, span), stats_active, stats_resting, state_now)

    def both_on(acc_now, kv_block, first_key, log_norm, row_delta):
        span = kv_block.shape[0]
        key_pos, key_doc = key_info(first_key, span)

        def both_active(acc_in):
            weights_low, grad_scores = gradient_terms(
                query_heads,
                grad_heads,
                kv_block[:, :head_dim],
                kv_block[:, head_dim:],
                log_norm,
                row_delta,
                row_pos,
                row_doc,
                key_pos,
                key_doc,
            )
            return (
                acc_in + query_part(grad_scores, kv_block[:, :head_dim]),
                key_value_part(weights_low, grad_scores, query_heads, grad_heads),
            )

        def both_resting(acc_in):
            return (acc_in, jnp.zeros((span, 2 * head_dim), jnp.float32))

        return lax.cond(reaches(first_key, span), both_active, both_resting, acc_now)

    pack = lax.all_gather(own_block, "srv", axis=0, tiled=True)
    pack_rows = pack.shape[0]
    block_rows = min(512, pack_rows)

    def pack_stats(block_index, state_now):
        first_key = block_index * block_rows
        return stats_on(
            state_now, lax.dynamic_slice_in_dim(pack, first_key, block_rows, 0), first_key
        )

    final_state = lax.fori_loop(0, pack_rows // block_rows, pack_stats, start_state)
    run_max, run_sum, run_acc = final_state
    log_norm = run_max + jnp.log(run_sum)
    row_delta = run_acc / run_sum

    def pack_grads(block_index, carried):
        acc_now, terms_now = carried
        first_key = block_index * block_rows
        acc_new, part_new = both_on(
            acc_now,
            lax.dynamic_slice_in_dim(pack, first_key, block_rows, 0),
            first_key,
            log_norm,
            row_delta,
        )
        return (acc_new, lax.dynamic_update_slice_in_dim(terms_now, part_new, first_key, 0))

    query_acc, kv_terms = lax.fori_loop(
        0,
        pack_rows // block_rows,
        pack_grads,
        (zero_acc, jnp.zeros((pack_rows, 2 * head_dim), jnp.float32)),
    )
    kv_grads = lax.psum_scatter(kv_terms, "srv", scatter_dimension=0, tiled=True)
    grad_query = (
        (query_acc * head_dim ** (-0.5))
        .reshape(row_count, heads_here * head_dim)
        .astype(jnp.bfloat16)
    )
    current = kv_grads.reshape(row_count, 2, share, head_dim // share)
    member = lax.axis_index("grp") % share
    for bit_number in reversed(range(share.bit_length() - 1)):
        half_width = current.shape[2] // 2
        lower = current[:, :, :half_width]
        upper = current[:, :, half_width:]
        upper_side = member >> bit_number & 1 == 1
        keep_part = jnp.where(upper_side, upper, lower)
        send_part = jnp.where(upper_side, lower, upper)
        current = keep_part + partner(send_part, "grp", bit_number)
    key_sum = current[:, 0, 0, :]
    value_sum = current[:, 1, 0, :]
    return (grad_query, key_sum.astype(jnp.bfloat16), value_sum.astype(jnp.bfloat16))


def solution(mesh):
    in_specs = (P("srv", "grp"), P("srv", None), P("srv", None), P("srv", "grp"), P())
    out_specs = (P("srv", "grp"), P("srv", "grp"), P("srv", "grp"))
    return jax.shard_map(
        on_device, mesh=mesh, in_specs=in_specs, out_specs=out_specs, check_vma=False
    )
```

profile of v0, /device:TPU:8, one launch (start us, length us, event | category | flops | bytes accessed | tf_op | source)
XLA Modules:
  0.0 482.5 jit_solution(1550506052433006060)
XLA Ops:
  11.9 90.0 %all-gather.2.cloned.1.call-done = bf16[8192,256]{1,0:T(8,128)(2,1)} async-done(((bf16[256,256]{1,0:T(8,128)(2,1)}), bf16[8192,256]{1,0:T(8,128)(2,1)}) %all-gather.2.cloned.1.call-update) | async-done | bytes 4194320 | tf_op jit(solution)/shard_map/all_gather | solution.py:172
  101.9 60.3 %while.45 = (s32[]{:T(128)}, f32[2,256]{1,0:T(2,128)S(1)}, f32[2,256]{1,0:T(2,128)S(1)}, f32[2,256]{1,0:T(2,128)S(1)}, s32[]{:T(128)}, /*index=5*/s32[8192]{0:T(...) while((s32[]{:T(128)}, f32[2,256]{1,0:T(2,128)S(1)}, ...), condition=%wide.region_6.7_spmd.clone, body=%wide.region_0.6_spmd.clone.sunk | while | flops 137234704 | bytes 4251099 | solution.py:182
  105.2 3.8 conditional.6
  109.0 1.3 dynamic_slice.94
  112.3 3.8 conditional.6
  116.1 1.3 dynamic_slice.94
  119.4 1.3 dynamic_slice.94
  122.7 1.3 dynamic_slice.94
  126.0 1.3 dynamic_slice.94
  129.3 1.3 dynamic_slice.94
  132.6 1.3 dynamic_slice.94
  135.9 1.3 dynamic_slice.94
  139.2 1.3 dynamic_slice.94
  142.5 1.3 dynamic_slice.94
  155.7 1.3 dynamic_slice.94
  162.3 4.2 broadcast_in_dim.64
  166.5 73.1 %while.46 = (s32[]{:T(128)}, f32[256,2,128]{2,0,1:T(8,128)S(1)}, f32[8192,256]{0,1:T(8,128)}, s32[]{:T(128)}, s32[8192]{0:T(1024)}, /*index=5*/s32[256]{0:T(256)...) while((s32[]{:T(128)}, f32[256,2,128]{2,0,1:T(8,128)S(1)}, ...), condition=%wide.region_10.11_spmd.clone, body=%wide.region_7.10_spmd.clone.sunk | while | flops 338035456 | bytes 9070019 | solution.py:199
  169.5 5.4 %conditional.7 = (f32[256,2,128]{2,0,1:T(8,128)S(1)}, f32[512,256]{0,1:T(8,128)S(1)}) conditional(s32[]{:T(128)} %convert_element_type.66, f32[256,2,128]{2,0,1:T(8,128)S(1)} %get-tuple-element.1351, (s32[256]{0:T(256)S(1)}, s32[8192]{0:T(1024)}, s32[]{:T(128)}, s32[]{:T(128)}, s32[512]{0:T(512)S(1)}, /*index=5*/s32[]{:T(128)}, ...), branch_computations={%region_8.8_spmd, %region_9.9_spmd} | conditional | flops 338035456 | bytes 8017452 | solution.py:170
  178.7 5.4 %conditional.7 = (f32[256,2,128]{2,0,1:T(8,128)S(1)}, f32[512,256]{0,1:T(8,128)S(1)}) conditional(s32[]{:T(128)} %convert_element_type.66, f32[256,2,128]{2,0,1:T(8,128)S(1)} %get-tuple-element.1351, (s32[256]{0:T(256)S(1)}, s32[8192]{0:T(1024)}, s32[]{:T(128)}, s32[]{:T(128)}, s32[512]{0:T(512)S(1)}, /*index=5*/s32[]{:T(128)}, ...), branch_computations={%region_8.8_spmd, %region_9.9_spmd} | conditional | flops 338035456 | bytes 8017452 | solution.py:170
  239.7 218.0 %reduce-scatter.2.cloned.1.call-done = f32[256,256]{0,1:T(8,128)} async-done(((f32[8192,256]{0,1:T(8,128)}), f32[256,256]{0,1:T(8,128)}) %reduce-scatter.2.cloned.1.call-update) | async-done | bytes 262160 | tf_op jit(solution)/shard_map/reduce_scatter | solution.py:205
  458.7 4.2 collective-permute-start
  462.9 4.9 %collective-permute-done = f32[256,2,2,32]{0,3,2,1:T(8,128)S(1)} collective-permute-done((f32[256,2,2,32]{0,3,2,1:T(8,128)S(1)}, f32[256,2,2,32]{0,3,2,1:T(8,128)S(1)}, u32[]{:S(2)}, u32[]{:S(2)}) %collective-permute-start) | collective-permute-done | bytes 131104 | tf_op jit(solution)/shard_map/ppermute | solution.py:19
  468.9 2.5 collective-permute-start.1
  472.0 3.0 collective-permute-done.1
  (237 shorter events, 85.9 us)
Async XLA Ops:
  7.2 94.8 %all-gather.2.cloned.1.call-start = ((), (), s32[]{:S(2)}) async-start(), calls=%async_computation.1 | async-start | bytes 4325376 | tf_op jit(solution)/shard_map/all_gather | solution.py:172
  8.8 448.9 %reduce-scatter.2.cloned.1.call-start = ((), (), s32[]{:S(2)}) async-start(), calls=%async_computation.2 | async-start | bytes 8650752 | tf_op jit(solution)/shard_map/reduce_scatter | solution.py:205
  458.7 9.2 %collective-permute-start = (f32[256,2,2,32]{0,3,2,1:T(8,128)S(1)}, f32[256,2,2,32]{0,3,2,1:T(8,128)S(1)}, u32[]{:S(2)}, u32[]{:S(2)}) collective-permute-start(f32[256,2,2,32]{0,3,2,1:T(8,128)S(1)} %slice_select_fusion), channel_id=1, source_target_pairs={{0,64},{64,0},{32,96},{96,32},{128,192},{192,128},{160,224},{224,1... | collective-permute-start | bytes 393224 | tf_op jit(solution)/shard_map/ppermute | solution.py:19
  468.9 6.2 %collective-permute-start.1 = (f32[256,2,1,32]{0,3,2,1:T(8,128)S(1)}, f32[256,2,1,32]{0,3,2,1:T(8,128)S(1)}, u32[]{:S(2)}, u32[]{:S(2)}) collective-permute-start(f32[256,2,1,32]{0,3,2,1:T(8,128)S(1)} %slice_select_fusion.1), channel_id=1, source_target_pairs={{0,32},{32,0},{64,96},{96,64},{128,160},{160,128},{192,224},{224,1... | collective-permute-start | bytes 196616 | tf_op jit(solution)/shard_map/ppermute | solution.py:19
Sparse Core Ops, SparseCore 0:
  12.9 89.0 all-gather.1
  239.8 217.8 reduce-scatter.1
where the time goes:
time: 486 us; the launch traced here: 482 us
  waiting for transfers between devices  316 us (65%)
  local copies, waits for them, and re-layouts  85 us (17%)
  loops' own time  42.1 us (9%)
  between operations  14.2 us (3%)
  matrix products  13.7 us (3%)
  starting transfers between devices  6.8 us (1%)
    reduce_scatter x1, waiting for transfers between devices, on_device(): lax.psum_scatter(kv_terms, 'srv', scatter_dimension=0, tiled=True)  218 us
    all_gather x1, waiting for transfers between devices, on_device(): pack = lax.all_gather(own_block, 'srv', axis=0, tiled=True)  90 us
    dynamic_slice x32, local copies, waits for them, and re-layouts, reaches(): last_doc = lax.dynamic_slice_in_dim(doc_ids, first_key + span - 1, 1)[0]  41.3 us
    another operation x1, loops' own time, on_device(): lax.fori_loop(0, pack_rows // block_rows, pack_stats, start_state)  21.9 us
    another operation x1, loops' own time, on_device(): lax.fori_loop(0, pack_rows // block_rows, pack_grads, (zero_acc, jnp.zero...  19.2 us
    slice x32, local copies, waits for them, and re-layouts, reaches(): return (first_key <= row_last) & (last_doc >= row_doc[0])  17.3 us
    dynamic_update_slice x16, local copies, waits for them, and re-layouts, pack_grads(): lax.dynamic_update_slice_in_dim(terms_now, part_new, first_key, 0)  13.7 us
  transfers between devices with their start and end apart: 4, of which 4 were waited for; matrix products, arithmetic and copies ran while one was open for 1% of the time, Pallas kernels for 0%

commit v1 on v0

v1 whole, which is shorter than its diff:
```python
import functools
import math

import jax
import jax.numpy as jnp
from jax import lax
from jax.experimental import pallas as pl
from jax.experimental.pallas import tpu as pltpu
from jax.sharding import PartitionSpec as P

HD = 128
SIDE = 4
REACH = 9
HIDDEN = -1e30
MESH = pl.DeviceIdType.MESH
SCALE = HD ** -0.5
SCALE2 = SCALE * math.log2(math.e)


def kernel(
    share, q_ref, k_ref, v_ref, o_ref, doc_ref,
    dq_out, dk_out, dv_out,
    kv, qc, oc, qt, ot, low, high, prob, dprob, mrun, stat, stat_in,
    dqt, dq_in, part, got, accf, xout, xin, zown, zout, zin,
    loc_sem, qs_sem, qr_sem, ks_sem, kr_sem, ss_sem, sr_sem, ps_sem, pr_sem,
    xs_sem, xr_sem, zs_sem, zr_sem, ds_sem, dr_sem,
):
    R = q_ref.shape[0]
    grp = lax.axis_index("grp")
    srv = lax.axis_index("srv")
    core = lax.rem(srv, 2)
    chip = lax.div(srv, 2)
    y = lax.rem(chip, SIDE)
    x = lax.div(chip, SIDE)
    member = lax.rem(grp, share)
    kv_head = lax.div(grp, share)
    mate = srv + 1 - 2 * core

    def at(cx, cy):
        return (grp, (cx * SIDE + cy) * 2 + core)

    def remote(src, dst, ssem, rsem, device):
        return pltpu.make_async_remote_copy(
            src_ref=src, dst_ref=dst, send_sem=ssem, recv_sem=rsem,
            device_id=device, device_id_type=MESH,
        )

    col = pl.ds(pl.multiple_of(kv_head * HD, HD), HD)
    mine = pl.multiple_of(core * (2 * R), 2 * R)
    local = [
        pltpu.make_async_copy(k_ref.at[:, col], kv.at[0, :, pl.ds(0, HD)], loc_sem.at[0]),
        pltpu.make_async_copy(v_ref.at[:, col], kv.at[0, :, pl.ds(HD, HD)], loc_sem.at[1]),
    ]
    for h in range(2):
        rows = pl.ds(mine + h * R, R)
        cols = pl.ds(h * HD, HD)
        local.append(pltpu.make_async_copy(q_ref.at[:, cols], qc.at[rows], loc_sem.at[2 + 2 * h]))
        local.append(pltpu.make_async_copy(o_ref.at[:, cols], oc.at[rows], loc_sem.at[3 + 2 * h]))
    for copy in local:
        copy.start()

    barrier = pltpu.get_barrier_semaphore()

    def greet(device):
        pl.semaphore_signal(barrier, inc=1, device_id=device, device_id_type=MESH)

    far_out = (chip == 3) & (core == 1)
    far_in = (chip == 12) & (core == 1)
    greet((grp, mate))
    for e in range(1, SIDE):
        greet(at(x, lax.rem(y + e, SIDE)))
        greet(at(lax.rem(x + e, SIDE), y))
    for e in range(1, share):
        greet((grp - member + lax.rem(member + e, share), srv))

    @pl.when(far_out)
    def _():
        greet(at(3, 0))

    @pl.when(far_in)
    def _():
        greet(at(0, 3))

    wide = doc_ref.shape[1]
    number = lax.broadcasted_iota(jnp.int32, (32, wide), 0)
    count = jnp.zeros((32, wide), jnp.int32)
    for r in range(doc_ref.shape[0]):
        count = count + (doc_ref[pl.ds(r, 1), :] < number).astype(jnp.int32)
    first = jnp.sum(count, axis=1, keepdims=True)
    lane = lax.broadcasted_iota(jnp.int32, (1, wide), 1)
    per = R // wide
    for b in range(2):
        for t in range(per):
            row = (chip * 2 + b) * per + t
            own = doc_ref[pl.ds(row, 1), :]
            begin = jnp.sum(jnp.where(own == number, first, 0), axis=0, keepdims=True)
            for h in range(2):
                sl = pl.ds(b * 2 * R + h * R + t * wide, wide)
                low[:, sl] = begin
                high[:, sl] = lane + row * wide

    stat[0:1, :] = jnp.full((1, 4 * R), HIDDEN, jnp.float32)
    stat[1:3, :] = jnp.zeros((2, 4 * R), jnp.float32)
    dqt[...] = jnp.zeros_like(dqt)

    far = jnp.where(far_out | far_in, 1, 0)
    pl.semaphore_wait(barrier, 1 + 2 * (SIDE - 1) + share - 1 + far)

    for copy in local[:2]:
        copy.wait()

    def kv_send(slot, d, n, device):
        return remote(kv.at[slot], kv.at[d], ks_sem.at[n], kr_sem.at[d], device)

    own_sends = []
    for e in range(1, 3):
        own_sends.append((x + e < SIDE, kv_send(0, 4 * e, e - 1, at(lax.rem(x + e, SIDE), y))))
    own_sends.append((far_out, kv_send(0, 9, 2, at(3, 0))))
    for e in range(1, SIDE):
        own_sends.append((y + e < SIDE, kv_send(0, e, 2 + e, at(x, lax.rem(y + e, SIDE)))))
    near_sends = []
    for e in range(1, SIDE):
        near_sends.append(
            (x >= 1, kv_send(4, lax.rem(y + e, SIDE) - y + 4, 5 + e, at(x, lax.rem(y + e, SIDE))))
        )
    next_sends = []
    for e in range(1, SIDE):
        wraps = y + e >= SIDE
        cond = (x >= 2) & (wraps | (core == 1) if e == 1 else wraps)
        next_sends.append(
            (cond, kv_send(8, lax.rem(lax.rem(y + e, SIDE) - y + 8, 10), 8 + e, at(x, lax.rem(y + e, SIDE))))
        )

    def start_all(sends):
        for cond, copy in sends:
            pl.when(cond)(copy.start)

    start_all(own_sends)
    for copy in local[2:]:
        copy.wait()
    q_swap = remote(qc.at[pl.ds(mine, 2 * R)], qc.at[pl.ds(mine, 2 * R)], qs_sem.at[0], qr_sem.at[0], (grp, mate))
    o_swap = remote(oc.at[pl.ds(mine, 2 * R)], oc.at[pl.ds(mine, 2 * R)], qs_sem.at[1], qr_sem.at[1], (grp, mate))
    q_swap.start()
    o_swap.start()
    q_swap.wait()
    o_swap.wait()
    qt[...] = qc[...].T
    ot[...] = oc[...].T

    def kv_arrived(d):
        remote(kv.at[d], kv.at[d], ks_sem.at[0], kr_sem.at[d], (grp, mate)).wait_recv()

    row_in_block = lax.broadcasted_iota(jnp.int32, (R, R), 0)

    def stats_step(d, carry):
        @pl.when((d == 1) & (x >= 1))
        def _():
            kv_arrived(4)
            start_all(near_sends)

        @pl.when((d == 3) & (x >= 2))
        def _():
            kv_arrived(8)
            start_all(next_sends)

        @pl.when(chip >= d)
        def _():
            @pl.when(lax.rem(d, 4) != 0)
            def _():
                kv_arrived(d)

            key_pos = row_in_block + ((chip - d) * 2 + core) * R
            keys = kv[d, :, 0:HD]
            values = kv[d, :, HD:2 * HD]
            for g in range(4):
                sl = slice(g * R, (g + 1) * R)
                s = jnp.dot(keys, qt[:, sl], preferred_element_type=jnp.float32) * SCALE2
                ok = (key_pos >= low[:, sl]) & (key_pos <= high[:, sl])
                s = jnp.where(ok, s, HIDDEN)
                m_old = stat[0:1, sl]
                m_new = jnp.maximum(m_old, jnp.max(s, axis=0, keepdims=True))
                alpha = jnp.exp2(m_old - m_new)
                p = jnp.exp2(s - m_new)
                dp = jnp.dot(values, ot[:, sl], preferred_element_type=jnp.float32)
                stat[0:1, sl] = m_new
                stat[1:2, sl] = stat[1:2, sl] * alpha + jnp.sum(p, axis=0, keepdims=True)
                stat[2:3, sl] = stat[2:3, sl] * alpha + jnp.sum(p * dp, axis=0, keepdims=True)
                mrun[d, :, sl] = m_new
                prob[d, :, sl] = p
                dprob[d, :, sl] = dp

        return carry

    lax.fori_loop(0, 9 + core, stats_step, 0)

    stat_swap = remote(stat, stat_in, ss_sem, sr_sem, (grp, mate))
    stat_swap.start()
    stat_swap.wait()
    m_all = jnp.maximum(stat[0:1, :], stat_in[0:1, :])
    here = jnp.exp2(stat[0:1, :] - m_all)
    there = jnp.exp2(stat_in[0:1, :] - m_all)
    total = stat[1:2, :] * here + stat_in[1:2, :] * there
    weighted = stat[2:3, :] * here + stat_in[2:3, :] * there
    stat[4:5, :] = m_all + jnp.log2(total)
    stat[5:6, :] = weighted / total

    def part_copy(d):
        owner = chip - d
        oy = lax.rem(owner, SIDE)
        a = x - lax.div(owner, SIDE)
        tx = x - 3 * lax.div(a, 3)
        return remote(part.at[d], got.at[a, y], ps_sem.at[d], pr_sem.at[a, y], at(tx, oy))

    def grads_step(i, carry):
        d = 8 + core - i

        @pl.when(chip >= d)
        def _():
            plow, slow = [], []
            for g in range(4):
                sl = slice(g * R, (g + 1) * R)
                factor = jnp.exp2(mrun[d, :, sl] - stat[4:5, sl])
                p = prob[d, :, sl] * factor
                plow.append(p.astype(jnp.bfloat16))
                slow.append((p * (dprob[d, :, sl] - stat[5:6, sl])).astype(jnp.bfloat16))
            keys = kv[d, :, 0:HD]
            for b in range(2):
                dqt[b] += lax.dot_general(
                    keys, jnp.concatenate(slow[2 * b:2 * b + 2], axis=1),
                    (((0,), (0,)), ((), ())), preferred_element_type=jnp.float32,
                )
            dk = jnp.dot(jnp.concatenate(slow, axis=1), qc[...], preferred_element_type=jnp.float32)
            dv = jnp.dot(jnp.concatenate(plow, axis=1), oc[...], preferred_element_type=jnp.float32)

            @pl.when(lax.rem(d, 4) == 0)
            def _():
                accf[lax.div(d, 4), :, 0:HD] = dk
                accf[lax.div(d, 4), :, HD:2 * HD] = dv

            @pl.when(lax.rem(d, 4) != 0)
            def _():
                part[d, :, 0:HD] = dk.astype(jnp.bfloat16)
                part[d, :, HD:2 * HD] = dv.astype(jnp.bfloat16)
                part_copy(d).start()

        return carry

    lax.fori_loop(0, 9 + core, grads_step, 0)

    dq_swap = remote(dqt.at[1 - core], dq_in, ds_sem, dr_sem, (grp, mate))
    dq_swap.start()

    def part_arrived(a, sy):
        remote(got.at[a, sy], got.at[a, sy], ps_sem.at[0], pr_sem.at[a, sy], (grp, mate)).wait_recv()

    def gather_row(a, e, cond):
        sy = lax.rem(y + e, SIDE)

        @pl.when(cond)
        def _():
            part_arrived(a, sy)
            accf[a] += got[a, sy].astype(jnp.float32)

    x_sends = []
    for a in (2, 1):
        for e in range(1, SIDE):
            wraps = y + e >= SIDE
            if a == 1:
                cond = x >= 1
            else:
                cond = (x >= 2) & (wraps | (core == 1) if e == 1 else wraps)
            gather_row(a, e, cond)
        copy = remote(xout.at[a - 1], xin.at[a - 1], xs_sem.at[a - 1], xr_sem.at[a - 1], at(lax.rem(x - a + SIDE, SIDE), y))
        x_sends.append((x >= a, copy))

        @pl.when(x >= a)
        def _():
            xout[a - 1] = accf[a].astype(jnp.bfloat16)
            copy.start()

    for e in range(1, SIDE):
        gather_row(0, e, y + e < SIDE)

    dq_swap.wait()
    mixed = dqt[core] + dq_in[...]
    for h in range(2):
        dq_out[:, h * HD:(h + 1) * HD] = (mixed[:, h * R:(h + 1) * R].T * SCALE).astype(jnp.bfloat16)

    for a in (1, 2):
        @pl.when(x + a < SIDE)
        def _():
            remote(xin.at[a - 1], xin.at[a - 1], xs_sem.at[0], xr_sem.at[a - 1], (grp, mate)).wait_recv()
            accf[0] += xin[a - 1].astype(jnp.float32)

    @pl.when(far_out)
    def _():
        part_arrived(3, 0)
        accf[0] += got[3, 0].astype(jnp.float32)

    wide_out = HD // share
    turned = accf[0].T
    for m in range(share):
        for s in range(2):
            piece = turned[s * HD + m * wide_out:s * HD + (m + 1) * wide_out, :]
            zown[m, s * wide_out:(s + 1) * wide_out, :] = piece
            zout[m, s * wide_out:(s + 1) * wide_out, :] = piece.astype(jnp.bfloat16)
    z_sends = []
    for e in range(1, share):
        to = lax.rem(member + e, share)
        z_sends.append(
            remote(zout.at[to], zin.at[member], zs_sem.at[to], zr_sem.at[member], (grp - member + to, srv))
        )
    for copy in z_sends:
        copy.start()
    result = zown[member]
    for e in range(1, share):
        sender = lax.rem(member + e, share)
        remote(zin.at[sender], zin.at[sender], zs_sem.at[0], zr_sem.at[sender], (grp, mate)).wait_recv()
        result = result + zin[sender].astype(jnp.float32)
    dk_out[...] = (result[0:wide_out].T * SCALE).astype(jnp.bfloat16)
    dv_out[...] = result[wide_out:2 * wide_out].T.astype(jnp.bfloat16)

    for cond, copy in own_sends + near_sends + next_sends + x_sends:
        pl.when(cond)(copy.wait_send)

    def parts_sent(d, carry):
        @pl.when((chip >= d) & (lax.rem(d, 4) != 0))
        def _():
            part_copy(d).wait_send()

        return carry

    lax.fori_loop(1, 9 + core, parts_sent, 0)
    for copy in z_sends:
        copy.wait_send()


def on_device(queries, key_rows, value_rows, grad_output, doc_ids):
    R = queries.shape[0]
    share = lax.axis_size("grp") // (key_rows.shape[1] // HD)
    wide = min(128, R)
    docs = doc_ids.reshape(-1, wide)
    bf, f32, i32 = jnp.bfloat16, jnp.float32, jnp.int32
    dma = pltpu.SemaphoreType.DMA
    scratch = [
        pltpu.VMEM((10, R, 2 * HD), bf),
        pltpu.VMEM((4 * R, HD), bf),
        pltpu.VMEM((4 * R, HD), bf),
        pltpu.VMEM((HD, 4 * R), bf),
        pltpu.VMEM((HD, 4 * R), bf),
        pltpu.VMEM((1, 4 * R), i32),
        pltpu.VMEM((1, 4 * R), i32),
        pltpu.VMEM((10, R, 4 * R), f32),
        pltpu.VMEM((10, R, 4 * R), f32),
        pltpu.VMEM((10, 1, 4 * R), f32),
        pltpu.VMEM((8, 4 * R), f32),
        pltpu.VMEM((8, 4 * R), f32),
        pltpu.VMEM((2, HD, 2 * R), f32),
        pltpu.VMEM((HD, 2 * R), f32),
        pltpu.VMEM((10, R, 2 * HD), bf),
        pltpu.VMEM((4, SIDE, R, 2 * HD), bf),
        pltpu.VMEM((3, R, 2 * HD), f32),
        pltpu.VMEM((2, R, 2 * HD), bf),
        pltpu.VMEM((2, R, 2 * HD), bf),
        pltpu.VMEM((share, 2 * HD // share, R), f32),
        pltpu.VMEM((share, 2 * HD // share, R), bf),
        pltpu.VMEM((share, 2 * HD // share, R), bf),
        dma((6,)), dma((2,)), dma((2,)), dma((12,)), dma((10,)), dma(()), dma(()),
        dma((10,)), dma((4, SIDE)), dma((2,)), dma((2,)), dma((share,)), dma((share,)),
        dma(()), dma(()),
    ]
    vmem = pl.BlockSpec(memory_space=pltpu.VMEM)
    hbm = pl.BlockSpec(memory_space=pl.ANY)
    return pl.pallas_call(
        functools.partial(kernel, share),
        out_shape=(
            jax.ShapeDtypeStruct((R, 2 * HD), bf),
            jax.ShapeDtypeStruct((R, HD // share), bf),
            jax.ShapeDtypeStruct((R, HD // share), bf),
        ),
        in_specs=[hbm, hbm, hbm, hbm, vmem],
        out_specs=(vmem, vmem, vmem),
        scratch_shapes=scratch,
        compiler_params=pltpu.CompilerParams(
            collective_id=0, has_side_effects=True, vmem_limit_bytes=48 * 1024 * 1024
        ),
    )(queries, key_rows, value_rows, grad_output, docs)


def solution(mesh):
    in_specs = (P("srv", "grp"), P("srv", None), P("srv", None), P("srv", "grp"), P())
    out_specs = (P("srv", "grp"), P("srv", "grp"), P("srv", "grp"))
    return jax.shard_map(
        on_device, mesh=mesh, in_specs=in_specs, out_specs=out_specs, check_vma=False
    )
```

time: 486 us -> 61.6 us (0.13)
  the two profiles are of different devices: /device:TPU:8 before, /device:TPU:26 now
where the time goes in v1:
time: 61.6 us; the launch traced here: 61.2 us
  Pallas kernels  53.9 us (88%)
  local copies, waits for them, and re-layouts  6.68 us (11%)
  between operations  0.65 us (1%)
    pallas_call x1, Pallas kernels, on_device(): pl.pallas_call(functools.partial(kernel, share), out_shape=(jax.ShapeDtyp...  53.9 us
    unnamed x11, local copies, waits for them, and re-layouts  5.3 us
    pallas_call x2, local copies, waits for them, and re-layouts, on_device(): pl.pallas_call(functools.partial(kernel, share), out_shape=(jax.ShapeDtyp...  1.39 us

profile of v1, /device:TPU:26, one launch (start us, length us, event | category | flops | bytes accessed | tf_op | source)
XLA Modules:
  0.0 61.2 jit_solution(16519841188136067667)
XLA Ops:
  0.6 0.0 copy-start
  0.6 1.0 %copy-done = bf16[256,1024]{1,0:T(8,128)(2,1)S(1)} copy-done((bf16[256,1024]{1,0:T(8,128)(2,1)S(1)}, bf16[256,1024]{1,0:T(8,128)(2,1)}, u32[]{:S(2)}) %copy-start) | copy-done | bytes 524312
  1.7 0.0 copy-start.1
  1.7 1.0 %copy-done.1 = bf16[256,1024]{1,0:T(8,128)(2,1)S(1)} copy-done((bf16[256,1024]{1,0:T(8,128)(2,1)S(1)}, bf16[256,1024]{1,0:T(8,128)(2,1)}, u32[]{:S(2)}) %copy-start.1) | copy-done | bytes 524312
  2.7 0.0 copy-start.2
  2.7 0.9 %copy-done.2 = bf16[256,256]{1,0:T(8,128)(2,1)S(1)} copy-done((bf16[256,256]{1,0:T(8,128)(2,1)S(1)}, bf16[256,256]{1,0:T(8,128)(2,1)}, u32[]{:S(2)}) %copy-start.2) | copy-done | bytes 131096
  3.6 0.0 copy-start.3
  3.6 0.9 %copy-done.3 = bf16[256,256]{1,0:T(8,128)(2,1)S(1)} copy-done((bf16[256,256]{1,0:T(8,128)(2,1)S(1)}, bf16[256,256]{1,0:T(8,128)(2,1)}, u32[]{:S(2)}) %copy-start.3) | copy-done | bytes 131096
  4.5 0.0 copy-start.4
  4.5 0.8 %copy-done.4 = s32[8192]{0:T(1024)S(1)} copy-done((s32[8192]{0:T(1024)S(1)}, s32[8192]{0:T(1024)}, u32[]{:S(2)}) %copy-start.4) | copy-done | bytes 32792
  5.3 53.9 %shard_map.76 = (bf16[256,256]{1,0:T(8,128)(2,1)S(1)}, bf16[256,32]{1,0:T(8,128)(2,1)S(1)}, bf16[256,32]{1,0:T(8,128)(2,1)S(1)}) custom-call(bf16[256,256]{1,0:T(8,128)(2,1)S(1)} %copy-done.2, bf16[256,1024]{1,0:T(8,128)(2,1)S(1)} %copy-done, bf16[256,1024]{1,0:T(8,128)(2,1)S(1)} %copy-done.1, bf16[256,256]{1,0:T(8,128)(2,1)S(1)} %copy-done.3, ...), custom_call_target="tpu_custom_call" | custom-call | tf_op jit(solution)/shard_map/pallas_call | solution.py:374
  59.2 0.7 %copy.8 = bf16[256,32]{0,1:T(8,128)(2,1)} copy(bf16[256,32]{1,0:T(8,128)(2,1)S(1)} %get-tuple-element.4) | data formatting | bytes 32768 | tf_op jit(solution)/shard_map/pallas_call | solution.py:374
  59.9 0.7 %copy.9 = bf16[256,32]{0,1:T(8,128)(2,1)} copy(bf16[256,32]{1,0:T(8,128)(2,1)S(1)} %get-tuple-element.5) | data formatting | bytes 32768 | tf_op jit(solution)/shard_map/pallas_call | solution.py:374
  60.6 0.7 %copy.11 = bf16[256,256]{1,0:T(8,128)(2,1)} copy(bf16[256,256]{1,0:T(8,128)(2,1)S(1)} %get-tuple-element.9) | data formatting | bytes 262144
Async XLA Ops:
  0.6 1.0 %copy-start = (bf16[256,1024]{1,0:T(8,128)(2,1)S(1)}, bf16[256,1024]{1,0:T(8,128)(2,1)}, u32[]{:S(2)}) copy-start(bf16[256,1024]{1,0:T(8,128)(2,1)} %k_ref.1) | copy-start | bytes 1572868
  1.7 1.0 %copy-start.1 = (bf16[256,1024]{1,0:T(8,128)(2,1)S(1)}, bf16[256,1024]{1,0:T(8,128)(2,1)}, u32[]{:S(2)}) copy-start(bf16[256,1024]{1,0:T(8,128)(2,1)} %v_ref.1) | copy-start | bytes 1572868
  2.7 0.9 %copy-start.2 = (bf16[256,256]{1,0:T(8,128)(2,1)S(1)}, bf16[256,256]{1,0:T(8,128)(2,1)}, u32[]{:S(2)}) copy-start(bf16[256,256]{1,0:T(8,128)(2,1)} %q_ref.1) | copy-start | bytes 393220
  3.6 0.9 %copy-start.3 = (bf16[256,256]{1,0:T(8,128)(2,1)S(1)}, bf16[256,256]{1,0:T(8,128)(2,1)}, u32[]{:S(2)}) copy-start(bf16[256,256]{1,0:T(8,128)(2,1)} %o_ref.1) | copy-start | bytes 393220
  4.5 0.8 %copy-start.4 = (s32[8192]{0:T(1024)S(1)}, s32[8192]{0:T(1024)}, u32[]{:S(2)}) copy-start(s32[8192]{0:T(1024)} %param.9) | copy-start | bytes 98308

commit v2 on v1

--- a/solution.py
+++ b/solution.py
@@ -21,9 +21,9 @@
     share, q_ref, k_ref, v_ref, o_ref, doc_ref,
     dq_out, dk_out, dv_out,
     kv, qc, oc, qt, ot, low, high, prob, dprob, mrun, stat, stat_in,
-    dqt, dq_in, part, got, accf, xout, xin, zown, zout, zin,
+    dqt, dq_in, part, got, accf, zown, zout, zin,
     loc_sem, qs_sem, qr_sem, ks_sem, kr_sem, ss_sem, sr_sem, ps_sem, pr_sem,
-    xs_sem, xr_sem, zs_sem, zr_sem, ds_sem, dr_sem,
+    zs_sem, zr_sem, ds_sem, dr_sem,
 ):
     R = q_ref.shape[0]
     grp = lax.axis_index("grp")
@@ -109,26 +109,38 @@
     for copy in local[:2]:
         copy.wait()
 
-    def kv_send(slot, d, n, device):
+    up, down = lax.rem(y + 1, SIDE), lax.rem(y + SIDE - 1, SIDE)
+    x_up, x_down = lax.rem(x + 1, SIDE), lax.rem(x + SIDE - 1, SIDE)
+    middle = (y == 1) | (y == 2)
+
+    def kv_send(n, slot, d, device):
         return remote(kv.at[slot], kv.at[d], ks_sem.at[n], kr_sem.at[d], device)
 
-    own_sends = []
-    for e in range(1, 3):
-        own_sends.append((x + e < SIDE, kv_send(0, 4 * e, e - 1, at(lax.rem(x + e, SIDE), y))))
-    own_sends.append((far_out, kv_send(0, 9, 2, at(3, 0))))
-    for e in range(1, SIDE):
-        own_sends.append((y + e < SIDE, kv_send(0, e, 2 + e, at(x, lax.rem(y + e, SIDE)))))
-    near_sends = []
-    for e in range(1, SIDE):
-        near_sends.append(
-            (x >= 1, kv_send(4, lax.rem(y + e, SIDE) - y + 4, 5 + e, at(x, lax.rem(y + e, SIDE))))
-        )
-    next_sends = []
-    for e in range(1, SIDE):
-        wraps = y + e >= SIDE
-        cond = (x >= 2) & (wraps | (core == 1) if e == 1 else wraps)
-        next_sends.append(
-            (cond, kv_send(8, lax.rem(lax.rem(y + e, SIDE) - y + 8, 10), 8 + e, at(x, lax.rem(y + e, SIDE))))
+    own_sends = [
+        (x < SIDE - 1, kv_send(0, 0, 4, at(x_up, y))),
+        (y < SIDE - 1, kv_send(1, 0, 1, at(x, up))),
+        (y == 0, kv_send(2, 0, 3, at(x, down))),
+        (far_out, kv_send(3, 0, 9, at(3, 0))),
+    ]
+    own_relay = [(middle, kv_send(4, 1, 2, at(x, up)))]
+    near_sends = [
+        ((x >= 1) & (x < SIDE - 1), kv_send(5, 4, 8, at(x_up, y))),
+        (x >= 1, kv_send(6, 4, 4 + up - y, at(x, up))),
+        (x >= 1, kv_send(7, 4, 4 + down - y, at(x, down))),
+    ]
+    near_slot = 4 + y - up
+    near_relay = [(x >= 1, kv_send(8, near_slot, 4 + down - up, at(x, down)))]
+    next_sends = [
+        ((x >= 2) & (y >= 1), kv_send(9, 8, 7, at(x, down))),
+        ((x >= 2) & (y == SIDE - 1), kv_send(10, 8, 5, at(x, up))),
+        ((x >= 2) & (y < SIDE - 1) & (core == 1), kv_send(11, 8, 9, at(x, up))),
+    ]
+    next_relay = [((x >= 2) & middle, kv_send(12, 7, 6, at(x, down)))]
+
+    def early(d):
+        return (
+            (d == 4) | (d == 8) | ((d == 1) & middle)
+            | ((d == 3) & (y < SIDE - 1)) | ((d == 7) & (y >= 1))
         )
 
     def start_all(sends):
@@ -153,19 +165,34 @@
     row_in_block = lax.broadcasted_iota(jnp.int32, (R, R), 0)
 
     def stats_step(d, carry):
+        @pl.when((d == 1) & middle)
+        def _():
+            kv_arrived(1)
+            start_all(own_relay)
+
         @pl.when((d == 1) & (x >= 1))
         def _():
             kv_arrived(4)
             start_all(near_sends)
 
+        @pl.when((d == 2) & (x >= 1))
+        def _():
+            kv_arrived(near_slot)
+            start_all(near_relay)
+
         @pl.when((d == 3) & (x >= 2))
         def _():
             kv_arrived(8)
             start_all(next_sends)
 
+        @pl.when((d == 5) & (x >= 2) & middle)
+        def _():
+            kv_arrived(7)
+            start_all(next_relay)
+
         @pl.when(chip >= d)
         def _():
-            @pl.when(lax.rem(d, 4) != 0)
+            @pl.when((d != 0) & jnp.logical_not(early(d)))
             def _():
                 kv_arrived(d)
 
@@ -208,8 +235,11 @@
         owner = chip - d
         oy = lax.rem(owner, SIDE)
         a = x - lax.div(owner, SIDE)
+        t = lax.rem(oy - y + SIDE, SIDE)
+        forward = (t == 1) | ((t == 2) & (a > 0))
+        ty = jnp.where((a == 3) | jnp.logical_not(forward), down, up)
         tx = x - 3 * lax.div(a, 3)
-        return remote(part.at[d], got.at[a, y], ps_sem.at[d], pr_sem.at[a, y], at(tx, oy))
+        return remote(part.at[d], got.at[4 * a + t], ps_sem.at[d], pr_sem.at[4 * a + t], at(tx, ty))
 
     def grads_step(i, carry):
         d = 8 + core - i
@@ -232,12 +262,14 @@
             dk = jnp.dot(jnp.concatenate(slow, axis=1), qc[...], preferred_element_type=jnp.float32)
             dv = jnp.dot(jnp.concatenate(plow, axis=1), oc[...], preferred_element_type=jnp.float32)
 
-            @pl.when(lax.rem(d, 4) == 0)
+            stays = (d == 0) | early(d)
+
+            @pl.when(stays)
             def _():
-                accf[lax.div(d, 4), :, 0:HD] = dk
-                accf[lax.div(d, 4), :, HD:2 * HD] = dv
-
-            @pl.when(lax.rem(d, 4) != 0)
+                accf[d, :, 0:HD] = dk
+                accf[d, :, HD:2 * HD] = dv
+
+            @pl.when(jnp.logical_not(stays))
             def _():
                 part[d, :, 0:HD] = dk.astype(jnp.bfloat16)
                 part[d, :, HD:2 * HD] = dv.astype(jnp.bfloat16)
@@ -250,52 +282,44 @@
     dq_swap = remote(dqt.at[1 - core], dq_in, ds_sem, dr_sem, (grp, mate))
     dq_swap.start()
 
-    def part_arrived(a, sy):
-        remote(got.at[a, sy], got.at[a, sy], ps_sem.at[0], pr_sem.at[a, sy], (grp, mate)).wait_recv()
-
-    def gather_row(a, e, cond):
-        sy = lax.rem(y + e, SIDE)
-
+    def add(d, slot, cond):
         @pl.when(cond)
         def _():
-            part_arrived(a, sy)
-            accf[a] += got[a, sy].astype(jnp.float32)
-
-    x_sends = []
-    for a in (2, 1):
-        for e in range(1, SIDE):
-            wraps = y + e >= SIDE
-            if a == 1:
-                cond = x >= 1
-            else:
-                cond = (x >= 2) & (wraps | (core == 1) if e == 1 else wraps)
-            gather_row(a, e, cond)
-        copy = remote(xout.at[a - 1], xin.at[a - 1], xs_sem.at[a - 1], xr_sem.at[a - 1], at(lax.rem(x - a + SIDE, SIDE), y))
-        x_sends.append((x >= a, copy))
-
-        @pl.when(x >= a)
-        def _():
-            xout[a - 1] = accf[a].astype(jnp.bfloat16)
+            remote(got.at[slot], got.at[slot], ps_sem.at[0], pr_sem.at[slot], (grp, mate)).wait_recv()
+            accf[d] += got[slot].astype(jnp.float32)
+
+    def pass_on(d, cond, copy):
+        @pl.when(cond)
+        def _():
+            part[d] = accf[d].astype(jnp.bfloat16)
             copy.start()
 
-    for e in range(1, SIDE):
-        gather_row(0, e, y + e < SIDE)
+    def x_copy(d, slot):
+        return remote(part.at[d], got.at[slot], ps_sem.at[d], pr_sem.at[slot], at(x_down, y))
+
+    add(7, 10, (x >= 2) & middle)
+    pass_on(7, (x >= 2) & middle, part_copy(7))
+    add(near_slot, 6, x >= 1)
+    pass_on(near_slot, x >= 1, part_copy(near_slot))
+    add(8, 9, (x >= 2) & (y >= 1))
+    add(8, 11, (x >= 2) & ((y == SIDE - 1) | (core == 1)))
+    pass_on(8, x >= 2, x_copy(8, 8))
+    add(1, 2, middle)
+    pass_on(1, middle, part_copy(1))
+    add(4, 7, x >= 1)
+    add(4, 5, x >= 1)
+    add(4, 8, (x >= 1) & (x < SIDE - 1))
+    pass_on(4, x >= 1, x_copy(4, 4))
+    add(0, 3, y < SIDE - 1)
+    add(0, 1, y == 0)
 
     dq_swap.wait()
     mixed = dqt[core] + dq_in[...]
     for h in range(2):
         dq_out[:, h * HD:(h + 1) * HD] = (mixed[:, h * R:(h + 1) * R].T * SCALE).astype(jnp.bfloat16)
 
-    for a in (1, 2):
-        @pl.when(x + a < SIDE)
-        def _():
-            remote(xin.at[a - 1], xin.at[a - 1], xs_sem.at[0], xr_sem.at[a - 1], (grp, mate)).wait_recv()
-            accf[0] += xin[a - 1].astype(jnp.float32)
-
-    @pl.when(far_out)
-    def _():
-        part_arrived(3, 0)
-        accf[0] += got[3, 0].astype(jnp.float32)
+    add(0, 4, x < SIDE - 1)
+    add(0, 15, far_out)
 
     wide_out = HD // share
     turned = accf[0].T
@@ -317,14 +341,15 @@
         sender = lax.rem(member + e, share)
         remote(zin.at[sender], zin.at[sender], zs_sem.at[0], zr_sem.at[sender], (grp, mate)).wait_recv()
         result = result + zin[sender].astype(jnp.float32)
-    dk_out[...] = (result[0:wide_out].T * SCALE).astype(jnp.bfloat16)
-    dv_out[...] = result[wide_out:2 * wide_out].T.astype(jnp.bfloat16)
-
-    for cond, copy in own_sends + near_sends + next_sends + x_sends:
-        pl.when(cond)(copy.wait_send)
+    dk_out[...] = (result[0:wide_out] * SCALE).astype(jnp.bfloat16)
+    dv_out[...] = result[wide_out:2 * wide_out].astype(jnp.bfloat16)
+
+    for sends in (own_sends, own_relay, near_sends, near_relay, next_sends, next_relay):
+        for cond, copy in sends:
+            pl.when(cond)(copy.wait_send)
 
     def parts_sent(d, carry):
-        @pl.when((chip >= d) & (lax.rem(d, 4) != 0))
+        @pl.when((chip >= d) & ((d != 4) | (x >= 1)) & ((d != 8) | (x >= 2)))
         def _():
             part_copy(d).wait_send()
 
@@ -358,33 +383,32 @@
         pltpu.VMEM((2, HD, 2 * R), f32),
         pltpu.VMEM((HD, 2 * R), f32),
         pltpu.VMEM((10, R, 2 * HD), bf),
-        pltpu.VMEM((4, SIDE, R, 2 * HD), bf),
-        pltpu.VMEM((3, R, 2 * HD), f32),
-        pltpu.VMEM((2, R, 2 * HD), bf),
-        pltpu.VMEM((2, R, 2 * HD), bf),
+        pltpu.VMEM((16, R, 2 * HD), bf),
+        pltpu.VMEM((10, R, 2 * HD), f32),
         pltpu.VMEM((share, 2 * HD // share, R), f32),
         pltpu.VMEM((share, 2 * HD // share, R), bf),
         pltpu.VMEM((share, 2 * HD // share, R), bf),
-        dma((6,)), dma((2,)), dma((2,)), dma((12,)), dma((10,)), dma(()), dma(()),
-        dma((10,)), dma((4, SIDE)), dma((2,)), dma((2,)), dma((share,)), dma((share,)),
+        dma((6,)), dma((2,)), dma((2,)), dma((13,)), dma((10,)), dma(()), dma(()),
+        dma((10,)), dma((16,)), dma((share,)), dma((share,)),
         dma(()), dma(()),
     ]
     vmem = pl.BlockSpec(memory_space=pltpu.VMEM)
-    hbm = pl.BlockSpec(memory_space=pl.ANY)
-    return pl.pallas_call(
+    hbm = pl.BlockSpec(memory_space=pltpu.HBM)
+    dq, dk, dv = pl.pallas_call(
         functools.partial(kernel, share),
         out_shape=(
             jax.ShapeDtypeStruct((R, 2 * HD), bf),
-            jax.ShapeDtypeStruct((R, HD // share), bf),
-            jax.ShapeDtypeStruct((R, HD // share), bf),
+            jax.ShapeDtypeStruct((HD // share, R), bf),
+            jax.ShapeDtypeStruct((HD // share, R), bf),
         ),
         in_specs=[hbm, hbm, hbm, hbm, vmem],
         out_specs=(vmem, vmem, vmem),
         scratch_shapes=scratch,
         compiler_params=pltpu.CompilerParams(
-            collective_id=0, has_side_effects=True, vmem_limit_bytes=48 * 1024 * 1024
+            collective_id=0, has_side_effects=True, vmem_limit_bytes=63 * 1024 * 1024
         ),
     )(queries, key_rows, value_rows, grad_output, docs)
+    return dq, dk.T, dv.T
 
 
 def solution(mesh):

time: 61.6 us -> 66.3 us (1.076)
  the two profiles are of different devices: /device:TPU:26 before, /device:TPU:18 now
where the time goes in v2:
time: 66.3 us; the launch traced here: 66 us
  Pallas kernels  62.4 us (94%)
  local copies, waits for them, and re-layouts  2.91 us (4%)
    pallas_call x1, Pallas kernels, on_device(): pl.pallas_call(functools.partial(kernel, share), out_shape=(jax.ShapeDtyp...  62.4 us
    unnamed x7, local copies, waits for them, and re-layouts  2.91 us

profile of v2, /device:TPU:18, one launch (start us, length us, event | category | flops | bytes accessed | tf_op | source)
XLA Modules:
  0.0 66.0 jit_solution(5967226445332958765)
XLA Ops:
  0.6 62.4 %shard_map.76 = (bf16[256,256]{1,0:T(8,128)(2,1)}, bf16[32,256]{1,0:T(8,128)(2,1)}, bf16[32,256]{1,0:T(8,128)(2,1)}) custom-call(bf16[256,256]{1,0:T(8,128)(2,1)} %q_ref.1, bf16[256,1024]{1,0:T(8,128)(2,1)} %k_ref.1, bf16[256,1024]{1,0:T(8,128)(2,1)} %v_ref.1, bf16[256,256]{1,0:T(8,128)(2,1)} %o_ref.1, s32[64,128]{1,0:T(8,128)} %bitcast.3), custom_call_target="tpu_custom_call" | custom-call | tf_op jit(solution)/shard_map/pallas_call | solution.py:397
  63.1 0.0 copy-start.1
  63.1 1.6 %copy.11 = bf16[256,256]{1,0:T(8,128)(2,1)} copy(bf16[256,256]{1,0:T(8,128)(2,1)} %get-tuple-element.12) | data formatting | bytes 262144
  64.7 0.0 copy-done.1
  64.7 0.0 copy-start
  64.7 0.6 copy.12
  65.3 0.1 copy-done
  65.4 0.6 copy.13
Async XLA Ops:
  63.1 1.6 %copy-start.1 = (bf16[32,256]{1,0:T(8,128)(2,1)S(1)}, bf16[32,256]{1,0:T(8,128)(2,1)}, u32[]{:S(2)}) copy-start(bf16[32,256]{1,0:T(8,128)(2,1)} %get-tuple-element.7) | copy-start | bytes 49156
  64.7 0.7 %copy-start = (bf16[32,256]{1,0:T(8,128)(2,1)S(1)}, bf16[32,256]{1,0:T(8,128)(2,1)}, u32[]{:S(2)}) copy-start(bf16[32,256]{1,0:T(8,128)(2,1)} %get-tuple-element.8) | copy-start | bytes 49156

commit v3 on v1

v3 whole, which is shorter than its diff:
```python
import functools
import math

import jax
import jax.numpy as jnp
from jax import lax
from jax.experimental import pallas as pl
from jax.experimental.pallas import tpu as pltpu
from jax.sharding import PartitionSpec as P

HD = 128
SIDE = 4
SLOTS = 7
HIDDEN = -1e30
MESH = pl.DeviceIdType.MESH
SCALE = HD ** -0.5
SCALE2 = SCALE * math.log2(math.e)


def kernel(
    share, q_ref, k_ref, v_ref, o_ref, doc_ref,
    dq_out, dk_out, dv_out,
    kv, qc, oc, qt, ot, low, high, prob, dprob, mrun, stat, stat_in, norm,
    dqt, dq_in, zq_out, zq_in, part, got, accf, xout, xin, zown, zout, zin, zsum,
    loc_sem, qs_sem, qr_sem, ks_sem, kr_sem, ss_sem, sr_sem, ps_sem, pr_sem,
    xs_sem, xr_sem, zs_sem, zr_sem, ds_sem, dr_sem,
):
    R = q_ref.shape[0]
    grp = lax.axis_index("grp")
    srv = lax.axis_index("srv")
    core = lax.rem(srv, 2)
    chip = lax.div(srv, 2)
    y = lax.rem(chip, SIDE)
    x = lax.div(chip, SIDE)
    member = lax.rem(grp, share)
    kv_head = lax.div(grp, share)
    plane = lax.rem(grp, 2)
    mate = (grp, srv + 1 - 2 * core)
    zmate = (grp + 1 - 2 * plane, srv)
    corner = (grp + 1 - 2 * plane, srv + 1 - 2 * core)
    side = lax.rem(x + y, 2)
    holds = side == plane
    column = lax.div(y, 2)

    def at(cx, cy):
        return (grp, (cx * SIDE + cy) * 2 + core)

    def remote(src, dst, ssem, rsem, device):
        return pltpu.make_async_remote_copy(
            src_ref=src, dst_ref=dst, send_sem=ssem, recv_sem=rsem,
            device_id=device, device_id_type=MESH,
        )

    col = pl.ds(pl.multiple_of(kv_head * HD, HD), HD)
    local_kv = [
        pltpu.make_async_copy(k_ref.at[:, col], kv.at[column, :, pl.ds(0, HD)], loc_sem.at[0]),
        pltpu.make_async_copy(v_ref.at[:, col], kv.at[column, :, pl.ds(HD, HD)], loc_sem.at[1]),
    ]
    local_q = []
    for h in range(2):
        rows = pl.ds(h * R, R)
        cols = pl.ds(h * HD, HD)
        local_q.append(pltpu.make_async_copy(q_ref.at[:, cols], qc.at[rows], loc_sem.at[2 + 2 * h]))
        local_q.append(pltpu.make_async_copy(o_ref.at[:, cols], oc.at[rows], loc_sem.at[3 + 2 * h]))
    for copy in local_kv:
        pl.when(holds)(copy.start)
    for copy in local_q:
        copy.start()

    barrier = pltpu.get_barrier_semaphore()

    def greet(device):
        pl.semaphore_signal(barrier, inc=1, device_id=device, device_id_type=MESH)

    far_out = (chip == 3) & (core == 1) & (plane == 1)
    far_in = (chip == 12) & (core == 1) & (plane == 1)
    greet(mate)
    greet(corner)
    for e in range(1, SIDE):
        greet(at(x, lax.rem(y + e, SIDE)))
        greet(at(lax.rem(x + e, SIDE), y))
    for e in range(1, share):
        greet((grp - member + lax.rem(member + e, share), srv))

    @pl.when(far_out)
    def _():
        greet(at(3, 0))

    @pl.when(far_in)
    def _():
        greet(at(0, 3))

    wide = doc_ref.shape[1]
    number = lax.broadcasted_iota(jnp.int32, (32, wide), 0)
    count = jnp.zeros((32, wide), jnp.int32)
    for r in range(doc_ref.shape[0]):
        count = count + (doc_ref[pl.ds(r, 1), :] < number).astype(jnp.int32)
    first = jnp.sum(count, axis=1, keepdims=True)
    lane = lax.broadcasted_iota(jnp.int32, (1, wide), 1)
    per = R // wide
    for b in range(2):
        block = chip * 2 + (core if b == 0 else 1 - core)
        for t in range(per):
            row = block * per + t
            own = doc_ref[pl.ds(row, 1), :]
            low[b:b + 1, t * wide:(t + 1) * wide] = jnp.sum(
                jnp.where(own == number, first, 0), axis=0, keepdims=True
            )
            high[b:b + 1, t * wide:(t + 1) * wide] = lane + row * wide

    stat[0:8, :] = jnp.full((8, R), HIDDEN, jnp.float32)
    stat[8:24, :] = jnp.zeros((16, R), jnp.float32)
    dqt[...] = jnp.zeros_like(dqt)

    far = jnp.where(far_out | far_in, 1, 0)
    pl.semaphore_wait(barrier, 2 + 2 * (SIDE - 1) + share - 1 + far)

    def swap(n, src, dst, device):
        return [
            remote(ref.at[pl.ds(src * 2 * R, 2 * R)], ref.at[pl.ds(dst * 2 * R, 2 * R)],
                   qs_sem.at[2 * n + i], qr_sem.at[2 * n + i], device)
            for i, ref in enumerate((qc, oc))
        ]

    to_core, to_plane, to_corner = swap(0, 0, 1, mate), swap(1, 0, 2, zmate), swap(2, 2, 3, mate)

    def kv_send(n, src, dst, device):
        return remote(kv.at[src], kv.at[dst], ks_sem.at[n], kr_sem.at[dst], device)

    own_sends, near_sends, next_sends = [], [], []
    for e in range(1, 3):
        own_sends.append(
            (holds & (x + e < SIDE), kv_send(e - 1, column, 2 * e + column, at(lax.rem(x + e, SIDE), y)))
        )
    own_sends.append((far_out, kv_send(2, column, 6, at(3, 0))))
    for e in range(1, SIDE):
        there = at(x, lax.rem(y + e, SIDE))
        wraps = y + e >= SIDE
        own_sends.append((holds & jnp.logical_not(wraps), kv_send(2 + e, column, column, there)))
        near_sends.append(
            (jnp.logical_not(holds) & (x >= 1), kv_send(5 + e, 2 + column, 2 + column, there))
        )
        reaches = wraps | (core == 1) if e == 1 else wraps
        next_sends.append((holds & (x >= 2) & reaches, kv_send(8 + e, 4 + column, 4 + column, there)))

    def start_all(sends):
        for cond, copy in sends:
            pl.when(cond)(copy.start)

    for copy in local_kv:
        pl.when(holds)(copy.wait)
    start_all(own_sends)
    for copy in local_q:
        copy.wait()
    for copy in to_plane + to_core:
        copy.start()
    for copy in to_core:
        copy.wait()
    for b in range(2):
        qt[:, b * 2 * R:(b + 1) * 2 * R] = qc[b * 2 * R:(b + 1) * 2 * R, :].T
        ot[:, b * 2 * R:(b + 1) * 2 * R] = oc[b * 2 * R:(b + 1) * 2 * R, :].T

    def kv_arrived(j):
        remote(kv.at[j], kv.at[j], ks_sem.at[0], kr_sem.at[j], mate).wait_recv()

    def slot(j):
        a = lax.div(j, 2)
        ky = jnp.where(a == 3, SIDE - 1, lax.rem(plane + x + a, 2) + 2 * lax.rem(j, 2))
        d = 4 * a + y - ky
        valid = (x >= a) & (d >= 0) & (d <= 8 + core) & ((a < 3) | (plane == 1))
        return a, ky, d, valid

    row_in_block = lax.broadcasted_iota(jnp.int32, (R, R), 0)

    def stats_block(z, j, d):
        key_pos = row_in_block + ((chip - d) * 2 + core) * R
        keys = kv[j, :, 0:HD]
        values = kv[j, :, HD:2 * HD]
        for g in range(4 * z, 4 * z + 4):
            b = (g // 2) % 2
            sl = slice(g * R, (g + 1) * R)
            s = jnp.dot(keys, qt[:, sl], preferred_element_type=jnp.float32) * SCALE2
            ok = (key_pos >= low[b:b + 1, :]) & (key_pos <= high[b:b + 1, :])
            s = jnp.where(ok, s, HIDDEN)
            m_old = stat[g:g + 1, :]
            m_new = jnp.maximum(m_old, jnp.max(s, axis=0, keepdims=True))
            alpha = jnp.exp2(m_old - m_new)
            p = jnp.exp2(s - m_new)
            dp = jnp.dot(values, ot[:, sl], preferred_element_type=jnp.float32)
            stat[g:g + 1, :] = m_new
            stat[8 + g:9 + g, :] = stat[8 + g:9 + g, :] * alpha + jnp.sum(p, axis=0, keepdims=True)
            stat[16 + g:17 + g, :] = stat[16 + g:17 + g, :] * alpha + jnp.sum(p * dp, axis=0, keepdims=True)
            mrun[j, g:g + 1, :] = m_new
            prob[j, :, sl] = p
            dprob[j, :, sl] = dp

    def stats_step(j, carry):
        @pl.when((j == 1) & (x >= 1) & jnp.logical_not(holds))
        def _():
            kv_arrived(2 + column)
            start_all(near_sends)

        @pl.when((j == 2) & (x >= 2) & holds)
        def _():
            kv_arrived(4 + column)
            start_all(next_sends)

        a, ky, d, valid = slot(j)

        @pl.when(valid)
        def _():
            @pl.when(ky != y)
            def _():
                kv_arrived(j)

            stats_block(0, j, d)

        return carry

    lax.fori_loop(0, SLOTS, stats_step, 0)

    for copy in to_plane:
        copy.wait()
    for copy in to_corner:
        copy.start()
    for copy in to_corner:
        copy.wait()
    for b in range(2, 4):
        qt[:, b * 2 * R:(b + 1) * 2 * R] = qc[b * 2 * R:(b + 1) * 2 * R, :].T
        ot[:, b * 2 * R:(b + 1) * 2 * R] = oc[b * 2 * R:(b + 1) * 2 * R, :].T

    def stats_other(j, carry):
        a, ky, d, valid = slot(j)

        @pl.when(valid)
        def _():
            stats_block(1, j, d)

        return carry

    lax.fori_loop(0, SLOTS, stats_other, 0)

    peers = (mate, zmate, corner)
    swaps = [remote(stat, stat_in.at[i], ss_sem.at[i], sr_sem.at[i], peers[i]) for i in range(3)]
    for copy in swaps:
        copy.start()
    for copy in swaps:
        copy.wait()
    for r in range(4):
        def rows_of(kind, r=r):
            mine = [stat[8 * kind + 2 * r:8 * kind + 2 * r + 2, :]]
            for i in range(3):
                there = 8 * kind + 2 * (r ^ (i + 1))
                mine.append(stat_in[i, there:there + 2, :])
            return mine

        tops = rows_of(0)
        top = jnp.maximum(jnp.maximum(tops[0], tops[1]), jnp.maximum(tops[2], tops[3]))
        factors = [jnp.exp2(t - top) for t in tops]
        total = sum(f * t for f, t in zip(factors, rows_of(1)))
        weighted = sum(f * t for f, t in zip(factors, rows_of(2)))
        norm[2 * r:2 * r + 2, :] = top + jnp.log2(total)
        norm[8 + 2 * r:8 + 2 * r + 2, :] = weighted / total

    def part_copy(j):
        a, ky, d, valid = slot(j)
        tx = x - 3 * lax.div(a, 3)
        return remote(part.at[j], got.at[a, y], ps_sem.at[j], pr_sem.at[a, y], at(tx, ky))

    def grads_step(i, carry):
        j = SLOTS - 1 - i
        a, ky, d, valid = slot(j)

        @pl.when(valid)
        def _():
            plow, slow = [], []
            for g in range(8):
                sl = slice(g * R, (g + 1) * R)
                factor = jnp.exp2(mrun[j, g:g + 1, :] - norm[g:g + 1, :])
                p = prob[j, :, sl] * factor
                plow.append(p.astype(jnp.bfloat16))
                slow.append((p * (dprob[j, :, sl] - norm[8 + g:9 + g, :])).astype(jnp.bfloat16))
            keys = kv[j, :, 0:HD]
            dk = jnp.dot(jnp.concatenate(slow, axis=1), qc[...], preferred_element_type=jnp.float32)
            dv = jnp.dot(jnp.concatenate(plow, axis=1), oc[...], preferred_element_type=jnp.float32)

            @pl.when(ky == y)
            def _():
                accf[a, :, 0:HD] = dk
                accf[a, :, HD:2 * HD] = dv

            @pl.when(ky != y)
            def _():
                part[j, :, 0:HD] = dk.astype(jnp.bfloat16)
                part[j, :, HD:2 * HD] = dv.astype(jnp.bfloat16)
                part_copy(j).start()

            for r in range(4):
                dqt[r] += lax.dot_general(
                    keys, jnp.concatenate(slow[2 * r:2 * r + 2], axis=1),
                    (((0,), (0,)), ((), ())), preferred_element_type=jnp.float32,
                )

        return carry

    lax.fori_loop(0, SLOTS, grads_step, 0)

    dq_swaps = [
        remote(dqt.at[2 * i + 1], dq_in.at[i], ds_sem.at[i], dr_sem.at[i], mate) for i in range(2)
    ]
    for copy in dq_swaps:
        copy.start()
    for copy in dq_swaps:
        copy.wait()
    zq_out[...] = (dqt[2] + dq_in[1]).astype(jnp.bfloat16)
    zq_swap = remote(zq_out, zq_in, ds_sem.at[2], dr_sem.at[2], zmate)
    zq_swap.start()

    def part_arrived(a, sy):
        remote(got.at[a, sy], got.at[a, sy], ps_sem.at[0], pr_sem.at[a, sy], mate).wait_recv()

    def gather_row(a, e, cond):
        sy = lax.rem(y + e, SIDE)

        @pl.when(cond)
        def _():
            part_arrived(a, sy)
            accf[a] += got[a, sy].astype(jnp.float32)

    x_sends = []
    for a in (2, 1):
        here = (x >= a) & (holds if a == 2 else jnp.logical_not(holds))
        for e in range(1, SIDE):
            wraps = y + e >= SIDE
            if a == 1:
                cond = here
            else:
                cond = here & (wraps | (core == 1) if e == 1 else wraps)
            gather_row(a, e, cond)
        copy = remote(xout.at[a - 1], xin.at[a - 1], xs_sem.at[a - 1], xr_sem.at[a - 1], at(lax.rem(x - a + SIDE, SIDE), y))
        x_sends.append((here, copy))

        @pl.when(here)
        def _():
            xout[a - 1] = accf[a].astype(jnp.bfloat16)
            copy.start()

    for e in range(1, SIDE):
        gather_row(0, e, holds & (y + e < SIDE))

    zq_swap.wait()
    mixed = dqt[0] + dq_in[0] + zq_in[...].astype(jnp.float32)
    for h in range(2):
        dq_out[:, h * HD:(h + 1) * HD] = (mixed[:, h * R:(h + 1) * R].T * SCALE).astype(jnp.bfloat16)

    for a in (1, 2):
        @pl.when(holds & (x + a < SIDE))
        def _():
            remote(xin.at[a - 1], xin.at[a - 1], xs_sem.at[0], xr_sem.at[a - 1], mate).wait_recv()
            accf[0] += xin[a - 1].astype(jnp.float32)

    @pl.when(far_out)
    def _():
        part_arrived(3, 0)
        accf[0] += got[3, 0].astype(jnp.float32)

    wide_out = HD // share
    pair = lax.div(member, 2)
    z_sends = []
    for e in range(1, share):
        to = lax.rem(member + e, share)
        z_sends.append(
            remote(zout.at[to], zin.at[pair], zs_sem.at[to], zr_sem.at[pair], (grp - member + to, srv))
        )

    @pl.when(holds)
    def _():
        turned = accf[0].T
        for m in range(share):
            for s in range(2):
                piece = turned[s * HD + m * wide_out:s * HD + (m + 1) * wide_out, :]
                zown[m, s * wide_out:(s + 1) * wide_out, :] = piece
                zout[m, s * wide_out:(s + 1) * wide_out, :] = piece.astype(jnp.bfloat16)
        for copy in z_sends:
            copy.start()
        zsum[...] = zown[member]

    @pl.when(jnp.logical_not(holds))
    def _():
        zsum[...] = jnp.zeros_like(zsum)

    for w in range(share // 2):
        @pl.when(jnp.logical_not(holds & (pair == w)))
        def _():
            remote(zin.at[w], zin.at[w], zs_sem.at[0], zr_sem.at[w], mate).wait_recv()
            zsum[...] += zin[w].astype(jnp.float32)

    dk_out[...] = (zsum[0:wide_out, :] * SCALE).astype(jnp.bfloat16)
    dv_out[...] = zsum[wide_out:2 * wide_out, :].astype(jnp.bfloat16)

    for cond, copy in own_sends + near_sends + next_sends + x_sends:
        pl.when(cond)(copy.wait_send)

    def parts_sent(j, carry):
        a, ky, d, valid = slot(j)

        @pl.when(valid & (ky != y))
        def _():
            part_copy(j).wait_send()

        return carry

    lax.fori_loop(0, SLOTS, parts_sent, 0)
    for copy in z_sends:
        pl.when(holds)(copy.wait_send)


def on_device(queries, key_rows, value_rows, grad_output, doc_ids):
    R = queries.shape[0]
    share = lax.axis_size("grp") // (key_rows.shape[1] // HD)
    wide = min(128, R)
    docs = doc_ids.reshape(-1, wide)
    bf, f32, i32 = jnp.bfloat16, jnp.float32, jnp.int32
    dma = pltpu.SemaphoreType.DMA
    scratch = [
        pltpu.VMEM((SLOTS, R, 2 * HD), bf),
        pltpu.VMEM((8 * R, HD), bf),
        pltpu.VMEM((8 * R, HD), bf),
        pltpu.VMEM((HD, 8 * R), bf),
        pltpu.VMEM((HD, 8 * R), bf),
        pltpu.VMEM((2, R), i32),
        pltpu.VMEM((2, R), i32),
        pltpu.VMEM((SLOTS, R, 8 * R), f32),
        pltpu.VMEM((SLOTS, R, 8 * R), f32),
        pltpu.VMEM((SLOTS, 8, R), f32),
        pltpu.VMEM((24, R), f32),
        pltpu.VMEM((3, 24, R), f32),
        pltpu.VMEM((16, R), f32),
        pltpu.VMEM((4, HD, 2 * R), f32),
        pltpu.VMEM((2, HD, 2 * R), f32),
        pltpu.VMEM((HD, 2 * R), bf),
        pltpu.VMEM((HD, 2 * R), bf),
        pltpu.VMEM((SLOTS, R, 2 * HD), bf),
        pltpu.VMEM((4, SIDE, R, 2 * HD), bf),
        pltpu.VMEM((3, R, 2 * HD), f32),
        pltpu.VMEM((2, R, 2 * HD), bf),
        pltpu.VMEM((2, R, 2 * HD), bf),
        pltpu.VMEM((share, 2 * HD // share, R), f32),
        pltpu.VMEM((share, 2 * HD // share, R), bf),
        pltpu.VMEM((share // 2, 2 * HD // share, R), bf),
        pltpu.VMEM((2 * HD // share, R), f32),
        dma((6,)), dma((6,)), dma((6,)), dma((12,)), dma((SLOTS,)), dma((3,)), dma((3,)),
        dma((SLOTS,)), dma((4, SIDE)), dma((2,)), dma((2,)), dma((share,)), dma((share // 2,)),
        dma((3,)), dma((3,)),
    ]
    vmem = pl.BlockSpec(memory_space=pltpu.VMEM)
    hbm = pl.BlockSpec(memory_space=pltpu.HBM)
    dq, dk, dv = pl.pallas_call(
        functools.partial(kernel, share),
        out_shape=(
            jax.ShapeDtypeStruct((R, 2 * HD), bf),
            jax.ShapeDtypeStruct((HD // share, R), bf),
            jax.ShapeDtypeStruct((HD // share, R), bf),
        ),
        in_specs=[hbm, hbm, hbm, hbm, vmem],
        out_specs=(vmem, vmem, vmem),
        scratch_shapes=scratch,
        compiler_params=pltpu.CompilerParams(
            collective_id=0, has_side_effects=True, vmem_limit_bytes=63 * 1024 * 1024
        ),
    )(queries, key_rows, value_rows, grad_output, docs)
    return dq, dk.T, dv.T


def solution(mesh):
    in_specs = (P("srv", "grp"), P("srv", None), P("srv", None), P("srv", "grp"), P())
    out_specs = (P("srv", "grp"), P("srv", "grp"), P("srv", "grp"))
    return jax.shard_map(
        on_device, mesh=mesh, in_specs=in_specs, out_specs=out_specs, check_vma=False
    )
```

time: 61.6 us -> 58.8 us (0.955)
  the two profiles are of different devices: /device:TPU:26 before, /device:TPU:18 now
where the time goes in v3:
time: 58.8 us; the launch traced here: 58.4 us
  Pallas kernels  54.9 us (93%)
  local copies, waits for them, and re-layouts  2.91 us (5%)
  between operations  0.65 us (1%)
    pallas_call x1, Pallas kernels, on_device(): pl.pallas_call(functools.partial(kernel, share), out_shape=(jax.ShapeDtyp...  54.9 us
    unnamed x7, local copies, waits for them, and re-layouts  2.91 us

profile of v3, /device:TPU:18, one launch (start us, length us, event | category | flops | bytes accessed | tf_op | source)
XLA Modules:
  0.0 58.4 jit_solution(18152972979556390880)
XLA Ops:
  0.6 54.9 %shard_map.76 = (bf16[256,256]{1,0:T(8,128)(2,1)}, bf16[32,256]{1,0:T(8,128)(2,1)}, bf16[32,256]{1,0:T(8,128)(2,1)}) custom-call(bf16[256,256]{1,0:T(8,128)(2,1)} %q_ref.1, bf16[256,1024]{1,0:T(8,128)(2,1)} %k_ref.1, bf16[256,1024]{1,0:T(8,128)(2,1)} %v_ref.1, bf16[256,256]{1,0:T(8,128)(2,1)} %o_ref.1, s32[64,128]{1,0:T(8,128)} %bitcast.3), custom_call_target="tpu_custom_call" | custom-call | tf_op jit(solution)/shard_map/pallas_call | solution.py:458
  55.5 0.0 copy-start.1
  55.5 1.6 %copy.11 = bf16[256,256]{1,0:T(8,128)(2,1)} copy(bf16[256,256]{1,0:T(8,128)(2,1)} %get-tuple-element.12) | data formatting | bytes 262144
  57.1 0.0 copy-done.1
  57.1 0.0 copy-start
  57.1 0.6 %copy.12 = bf16[256,32]{0,1:T(8,128)(2,1)} copy(bf16[256,32]{0,1:T(8,128)(2,1)S(1)} %bitcast.5) | data formatting | bytes 32768
  57.7 0.1 copy-done
  57.8 0.6 %copy.13 = bf16[256,32]{0,1:T(8,128)(2,1)} copy(bf16[256,32]{0,1:T(8,128)(2,1)S(1)} %bitcast.4) | data formatting | bytes 32768
Async XLA Ops:
  55.5 1.6 %copy-start.1 = (bf16[32,256]{1,0:T(8,128)(2,1)S(1)}, bf16[32,256]{1,0:T(8,128)(2,1)}, u32[]{:S(2)}) copy-start(bf16[32,256]{1,0:T(8,128)(2,1)} %get-tuple-element.7) | copy-start | bytes 49156
  57.1 0.7 %copy-start = (bf16[32,256]{1,0:T(8,128)(2,1)S(1)}, bf16[32,256]{1,0:T(8,128)(2,1)}, u32[]{:S(2)}) copy-start(bf16[32,256]{1,0:T(8,128)(2,1)} %get-tuple-element.8) | copy-start | bytes 49156

commit v4 on v3

--- a/solution.py
+++ b/solution.py
@@ -18,9 +18,9 @@
 
 
 def kernel(
-    share, q_ref, k_ref, v_ref, o_ref, doc_ref,
+    share, q_ref, k_ref, v_ref, o_ref, doc_hbm,
     dq_out, dk_out, dv_out,
-    kv, qc, oc, qt, ot, low, high, prob, dprob, mrun, stat, stat_in, norm,
+    doc_ref, kv, qc, oc, qt, ot, low, high, prob, dprob, mrun, stat, stat_in, norm,
     dqt, dq_in, zq_out, zq_in, part, got, accf, xout, xin, zown, zout, zin, zsum,
     loc_sem, qs_sem, qr_sem, ks_sem, kr_sem, ss_sem, sr_sem, ps_sem, pr_sem,
     xs_sem, xr_sem, zs_sem, zr_sem, ds_sem, dr_sem,
@@ -62,6 +62,8 @@
         cols = pl.ds(h * HD, HD)
         local_q.append(pltpu.make_async_copy(q_ref.at[:, cols], qc.at[rows], loc_sem.at[2 + 2 * h]))
         local_q.append(pltpu.make_async_copy(o_ref.at[:, cols], oc.at[rows], loc_sem.at[3 + 2 * h]))
+    local_doc = pltpu.make_async_copy(doc_hbm, doc_ref, loc_sem.at[6])
+    local_doc.start()
     for copy in local_kv:
         pl.when(holds)(copy.start)
     for copy in local_q:
@@ -90,6 +92,7 @@
     def _():
         greet(at(0, 3))
 
+    local_doc.wait()
     wide = doc_ref.shape[1]
     number = lax.broadcasted_iota(jnp.int32, (32, wide), 0)
     count = jnp.zeros((32, wide), jnp.int32)
@@ -205,6 +208,13 @@
             kv_arrived(4 + column)
             start_all(next_sends)
 
+        @pl.when(j == 4)
+        def _():
+            for copy in to_plane:
+                copy.wait()
+            for copy in to_corner:
+                copy.start()
+
         a, ky, d, valid = slot(j)
 
         @pl.when(valid)
@@ -219,10 +229,6 @@
 
     lax.fori_loop(0, SLOTS, stats_step, 0)
 
-    for copy in to_plane:
-        copy.wait()
-    for copy in to_corner:
-        copy.start()
     for copy in to_corner:
         copy.wait()
     for b in range(2, 4):
@@ -267,9 +273,42 @@
         tx = x - 3 * lax.div(a, 3)
         return remote(part.at[j], got.at[a, y], ps_sem.at[j], pr_sem.at[a, y], at(tx, ky))
 
+    def part_arrived(a, sy):
+        remote(got.at[a, sy], got.at[a, sy], ps_sem.at[0], pr_sem.at[a, sy], mate).wait_recv()
+
+    def gather_row(a, e, cond):
+        sy = lax.rem(y + e, SIDE)
+
+        @pl.when(cond)
+        def _():
+            part_arrived(a, sy)
+            accf[a] += got[a, sy].astype(jnp.float32)
+
+    def x_hand_over(a):
+        for e in range(1, SIDE):
+            wraps = y + e >= SIDE
+            reaches = True if a == 1 else (wraps | (core == 1) if e == 1 else wraps)
+            gather_row(a, e, x_here[a] & reaches)
+
+        @pl.when(x_here[a])
+        def _():
+            xout[a - 1] = accf[a].astype(jnp.bfloat16)
+            x_copy[a].start()
+
+    x_here = {1: (x >= 1) & jnp.logical_not(holds), 2: (x >= 2) & holds}
+    x_copy = {
+        a: remote(xout.at[a - 1], xin.at[a - 1], xs_sem.at[a - 1], xr_sem.at[a - 1],
+                  at(lax.rem(x - a + SIDE, SIDE), y))
+        for a in (1, 2)
+    }
+
     def grads_step(i, carry):
         j = SLOTS - 1 - i
         a, ky, d, valid = slot(j)
+
+        @pl.when(j == 1)
+        def _():
+            x_hand_over(2)
 
         @pl.when(valid)
         def _():
@@ -310,48 +349,16 @@
     ]
     for copy in dq_swaps:
         copy.start()
+
+    x_hand_over(1)
     for copy in dq_swaps:
         copy.wait()
     zq_out[...] = (dqt[2] + dq_in[1]).astype(jnp.bfloat16)
     zq_swap = remote(zq_out, zq_in, ds_sem.at[2], dr_sem.at[2], zmate)
     zq_swap.start()
 
-    def part_arrived(a, sy):
-        remote(got.at[a, sy], got.at[a, sy], ps_sem.at[0], pr_sem.at[a, sy], mate).wait_recv()
-
-    def gather_row(a, e, cond):
-        sy = lax.rem(y + e, SIDE)
-
-        @pl.when(cond)
-        def _():
-            part_arrived(a, sy)
-            accf[a] += got[a, sy].astype(jnp.float32)
-
-    x_sends = []
-    for a in (2, 1):
-        here = (x >= a) & (holds if a == 2 else jnp.logical_not(holds))
-        for e in range(1, SIDE):
-            wraps = y + e >= SIDE
-            if a == 1:
-                cond = here
-            else:
-                cond = here & (wraps | (core == 1) if e == 1 else wraps)
-            gather_row(a, e, cond)
-        copy = remote(xout.at[a - 1], xin.at[a - 1], xs_sem.at[a - 1], xr_sem.at[a - 1], at(lax.rem(x - a + SIDE, SIDE), y))
-        x_sends.append((here, copy))
-
-        @pl.when(here)
-        def _():
-            xout[a - 1] = accf[a].astype(jnp.bfloat16)
-            copy.start()
-
     for e in range(1, SIDE):
         gather_row(0, e, holds & (y + e < SIDE))
-
-    zq_swap.wait()
-    mixed = dqt[0] + dq_in[0] + zq_in[...].astype(jnp.float32)
-    for h in range(2):
-        dq_out[:, h * HD:(h + 1) * HD] = (mixed[:, h * R:(h + 1) * R].T * SCALE).astype(jnp.bfloat16)
 
     for a in (1, 2):
         @pl.when(holds & (x + a < SIDE))
@@ -389,6 +396,11 @@
     def _():
         zsum[...] = jnp.zeros_like(zsum)
 
+    zq_swap.wait()
+    mixed = dqt[0] + dq_in[0] + zq_in[...].astype(jnp.float32)
+    for h in range(2):
+        dq_out[:, h * HD:(h + 1) * HD] = (mixed[:, h * R:(h + 1) * R].T * SCALE).astype(jnp.bfloat16)
+
     for w in range(share // 2):
         @pl.when(jnp.logical_not(holds & (pair == w)))
         def _():
@@ -398,7 +410,7 @@
     dk_out[...] = (zsum[0:wide_out, :] * SCALE).astype(jnp.bfloat16)
     dv_out[...] = zsum[wide_out:2 * wide_out, :].astype(jnp.bfloat16)
 
-    for cond, copy in own_sends + near_sends + next_sends + x_sends:
+    for cond, copy in own_sends + near_sends + next_sends + [(x_here[a], x_copy[a]) for a in (1, 2)]:
         pl.when(cond)(copy.wait_send)
 
     def parts_sent(j, carry):
@@ -413,6 +425,17 @@
     lax.fori_loop(0, SLOTS, parts_sent, 0)
     for copy in z_sends:
         pl.when(holds)(copy.wait_send)
+
+
+def write_out(a_ref, b_ref, c_ref, a_out, b_out, c_out, sem):
+    copies = [
+        pltpu.make_async_copy(src, dst, sem.at[i])
+        for i, (src, dst) in enumerate(((a_ref, a_out), (b_ref, b_out), (c_ref, c_out)))
+    ]
+    for copy in copies:
+        copy.start()
+    for copy in copies:
+        copy.wait()
 
 
 def on_device(queries, key_rows, value_rows, grad_output, doc_ids):
@@ -423,6 +446,7 @@
     bf, f32, i32 = jnp.bfloat16, jnp.float32, jnp.int32
     dma = pltpu.SemaphoreType.DMA
     scratch = [
+        pltpu.VMEM(docs.shape, i32),
         pltpu.VMEM((SLOTS, R, 2 * HD), bf),
         pltpu.VMEM((8 * R, HD), bf),
         pltpu.VMEM((8 * R, HD), bf),
@@ -449,7 +473,7 @@
         pltpu.VMEM((share, 2 * HD // share, R), bf),
         pltpu.VMEM((share // 2, 2 * HD // share, R), bf),
         pltpu.VMEM((2 * HD // share, R), f32),
-        dma((6,)), dma((6,)), dma((6,)), dma((12,)), dma((SLOTS,)), dma((3,)), dma((3,)),
+        dma((7,)), dma((6,)), dma((6,)), dma((12,)), dma((SLOTS,)), dma((3,)), dma((3,)),
         dma((SLOTS,)), dma((4, SIDE)), dma((2,)), dma((2,)), dma((share,)), dma((share // 2,)),
         dma((3,)), dma((3,)),
     ]
@@ -458,17 +482,24 @@
     dq, dk, dv = pl.pallas_call(
         functools.partial(kernel, share),
         out_shape=(
-            jax.ShapeDtypeStruct((R, 2 * HD), bf),
-            jax.ShapeDtypeStruct((HD // share, R), bf),
-            jax.ShapeDtypeStruct((HD // share, R), bf),
+            pltpu.VMEM((R, 2 * HD), bf),
+            pltpu.VMEM((HD // share, R), bf),
+            pltpu.VMEM((HD // share, R), bf),
         ),
-        in_specs=[hbm, hbm, hbm, hbm, vmem],
+        in_specs=[hbm, hbm, hbm, hbm, hbm],
         out_specs=(vmem, vmem, vmem),
         scratch_shapes=scratch,
         compiler_params=pltpu.CompilerParams(
-            collective_id=0, has_side_effects=True, vmem_limit_bytes=63 * 1024 * 1024
+            collective_id=0, has_side_effects=True, vmem_limit_bytes=56 * 1024 * 1024
         ),
-    )(queries, key_rows, value_rows, grad_output, docs)
+    )(*(pltpu.with_memory_space_constraint(t, pltpu.HBM) for t in (queries, key_rows, value_rows, grad_output, docs)))
+    dq, dk, dv = pl.pallas_call(
+        write_out,
+        out_shape=tuple(jax.ShapeDtypeStruct(part.shape, part.dtype) for part in (dq, dk, dv)),
+        in_specs=[vmem, vmem, vmem],
+        out_specs=(hbm, hbm, hbm),
+        scratch_shapes=[dma((3,))],
+    )(*(pltpu.with_memory_space_constraint(t, pltpu.VMEM) for t in (dq, dk, dv)))
     return dq, dk.T, dv.T
 
 

time: 58.8 us -> 54.5 us (0.927)
  the two profiles are of different devices: /device:TPU:18 before, /device:TPU:12 now
where the time goes in v4:
time: 54.5 us; the launch traced here: 54.3 us
  Pallas kernels  53.6 us (98%)
  between operations  0.64 us (1%)
    pallas_call x1, Pallas kernels, on_device(): pl.pallas_call(functools.partial(kernel, share), out_shape=(pltpu.VMEM((R...  52.9 us

profile of v4, /device:TPU:12, one launch (start us, length us, event | category | flops | bytes accessed | tf_op | source)
XLA Modules:
  0.0 54.3 jit_solution(15717972018994765769)
XLA Ops:
  0.6 52.9 %shard_map.76 = (bf16[256,256]{1,0:T(8,128)(2,1)S(1)}, bf16[32,256]{1,0:T(8,128)(2,1)S(1)}, bf16[32,256]{1,0:T(8,128)(2,1)S(1)}) custom-call(bf16[256,256]{1,0:T(8,128)(2,1)} %q_ref.1, bf16[256,1024]{1,0:T(8,128)(2,1)} %k_ref.1, bf16[256,1024]{1,0:T(8,128)(2,1)} %v_ref.1, bf16[256,256]{1,0:T(8,128)(2,1)} %o_ref.1, s32[64,128]{1,0:T(8,128)} %bitcast.3), custom_call_target="tpu_custom_call" | custom-call | tf_op jit(solution)/shard_map/pallas_call | solution.py:482
  53.6 0.7 %shard_map.77 = (bf16[256,256]{1,0:T(8,128)(2,1)}, bf16[32,256]{1,0:T(8,128)(2,1)}, bf16[32,256]{1,0:T(8,128)(2,1)}) custom-call(bf16[256,256]{1,0:T(8,128)(2,1)S(1)} %get-tuple-element.9.a_ref, bf16[32,256]{1,0:T(8,128)(2,1)S(1)} %get-tuple-element.10.b_ref, bf16[32,256]{1,0:T(8,128)(2,1)S(1)} %get-tuple-element.11.c_ref), custom_call_target="tpu_custom_call" | custom-call | tf_op jit(solution)/shard_map/pallas_call | solution.py:496

commit v5 on v4

--- a/solution.py
+++ b/solution.py
@@ -23,7 +23,7 @@
     doc_ref, kv, qc, oc, qt, ot, low, high, prob, dprob, mrun, stat, stat_in, norm,
     dqt, dq_in, zq_out, zq_in, part, got, accf, xout, xin, zown, zout, zin, zsum,
     loc_sem, qs_sem, qr_sem, ks_sem, kr_sem, ss_sem, sr_sem, ps_sem, pr_sem,
-    xs_sem, xr_sem, zs_sem, zr_sem, ds_sem, dr_sem,
+    xs_sem, xr_sem, zs_sem, zr_sem, ds_sem, dr_sem, in_sem,
 ):
     R = q_ref.shape[0]
     grp = lax.axis_index("grp")
@@ -76,13 +76,23 @@
 
     far_out = (chip == 3) & (core == 1) & (plane == 1)
     far_in = (chip == 12) & (core == 1) & (plane == 1)
-    greet(mate)
-    greet(corner)
+    everyone = [mate, corner]
     for e in range(1, SIDE):
-        greet(at(x, lax.rem(y + e, SIDE)))
-        greet(at(lax.rem(x + e, SIDE), y))
+        everyone += [at(x, lax.rem(y + e, SIDE)), at(lax.rem(x + e, SIDE), y)]
     for e in range(1, share):
-        greet((grp - member + lax.rem(member + e, share), srv))
+        everyone.append((grp - member + lax.rem(member + e, share), srv))
+
+    leader = (member == 0) & (srv == 0)
+    beside = ((member == 0) & (srv == 1)) | ((member == 1) & (srv == 0))
+    around = (
+        ((member == 0) & (core == 0) & (chip > 0) & ((x == 0) | (y == 0)))
+        | ((member == 1) & (srv == 1)) | ((member >= 2) & (srv == 0))
+    )
+
+    @pl.when(jnp.logical_not(leader))
+    def _():
+        for device in everyone:
+            greet(device)
 
     @pl.when(far_out)
     def _():
@@ -116,7 +126,12 @@
     dqt[...] = jnp.zeros_like(dqt)
 
     far = jnp.where(far_out | far_in, 1, 0)
-    pl.semaphore_wait(barrier, 2 + 2 * (SIDE - 1) + share - 1 + far)
+    pl.semaphore_wait(barrier, 2 + 2 * (SIDE - 1) + share - 1 + far - jnp.where(beside | around, 1, 0))
+
+    @pl.when(leader)
+    def _():
+        for device in everyone:
+            pl.semaphore_signal(in_sem, inc=1, device_id=device, device_id_type=MESH)
 
     def swap(n, src, dst, device):
         return [
@@ -155,6 +170,11 @@
     start_all(own_sends)
     for copy in local_q:
         copy.wait()
+
+    @pl.when(beside)
+    def _():
+        pl.semaphore_wait(in_sem, 1)
+
     for copy in to_plane + to_core:
         copy.start()
     for copy in to_core:
@@ -248,6 +268,11 @@
 
     peers = (mate, zmate, corner)
     swaps = [remote(stat, stat_in.at[i], ss_sem.at[i], sr_sem.at[i], peers[i]) for i in range(3)]
+
+    @pl.when(around)
+    def _():
+        pl.semaphore_wait(in_sem, 1)
+
     for copy in swaps:
         copy.start()
     for copy in swaps:
@@ -475,7 +500,7 @@
         pltpu.VMEM((2 * HD // share, R), f32),
         dma((7,)), dma((6,)), dma((6,)), dma((12,)), dma((SLOTS,)), dma((3,)), dma((3,)),
         dma((SLOTS,)), dma((4, SIDE)), dma((2,)), dma((2,)), dma((share,)), dma((share // 2,)),
-        dma((3,)), dma((3,)),
+        dma((3,)), dma((3,)), pltpu.SemaphoreType.REGULAR,
     ]
     vmem = pl.BlockSpec(memory_space=pltpu.VMEM)
     hbm = pl.BlockSpec(memory_space=pltpu.HBM)

time: 54.5 us -> 51.8 us (0.950)
  the two profiles are of different devices: /device:TPU:12 before, /device:TPU:8 now
where the time goes in v5:
time: 51.8 us; the launch traced here: 51.6 us
  Pallas kernels  51 us (98%)
  between operations  0.64 us (1%)
    pallas_call x1, Pallas kernels, on_device(): pl.pallas_call(functools.partial(kernel, share), out_shape=(pltpu.VMEM((R...  50.3 us

profile of v5, /device:TPU:8, one launch (start us, length us, event | category | flops | bytes accessed | tf_op | source)
XLA Modules:
  0.0 51.6 jit_solution(15097088756890081124)
XLA Ops:
  0.6 50.3 %shard_map.76 = (bf16[256,256]{1,0:T(8,128)(2,1)S(1)}, bf16[32,256]{1,0:T(8,128)(2,1)S(1)}, bf16[32,256]{1,0:T(8,128)(2,1)S(1)}) custom-call(bf16[256,256]{1,0:T(8,128)(2,1)} %q_ref.1, bf16[256,1024]{1,0:T(8,128)(2,1)} %k_ref.1, bf16[256,1024]{1,0:T(8,128)(2,1)} %v_ref.1, bf16[256,256]{1,0:T(8,128)(2,1)} %o_ref.1, s32[64,128]{1,0:T(8,128)} %bitcast.3), custom_call_target="tpu_custom_call" | custom-call | tf_op jit(solution)/shard_map/pallas_call | solution.py:507
  50.9 0.7 %shard_map.77 = (bf16[256,256]{1,0:T(8,128)(2,1)}, bf16[32,256]{1,0:T(8,128)(2,1)}, bf16[32,256]{1,0:T(8,128)(2,1)}) custom-call(bf16[256,256]{1,0:T(8,128)(2,1)S(1)} %get-tuple-element.9.a_ref, bf16[32,256]{1,0:T(8,128)(2,1)S(1)} %get-tuple-element.10.b_ref, bf16[32,256]{1,0:T(8,128)(2,1)S(1)} %get-tuple-element.11.c_ref), custom_call_target="tpu_custom_call" | custom-call | tf_op jit(solution)/shard_map/pallas_call | solution.py:521

commit v6 on v5

--- a/solution.py
+++ b/solution.py
@@ -20,7 +20,7 @@
 def kernel(
     share, q_ref, k_ref, v_ref, o_ref, doc_hbm,
     dq_out, dk_out, dv_out,
-    doc_ref, kv, qc, oc, qt, ot, low, high, prob, dprob, mrun, stat, stat_in, norm,
+    doc_ref, kv, qc, oc, qt, ot, marks, high, prob, dprob, mrun, gscore, stat, stat_in, norm,
     dqt, dq_in, zq_out, zq_in, part, got, accf, xout, xin, zown, zout, zin, zsum,
     loc_sem, qs_sem, qr_sem, ks_sem, kr_sem, ss_sem, sr_sem, ps_sem, pr_sem,
     xs_sem, xr_sem, zs_sem, zr_sem, ds_sem, dr_sem, in_sem,
@@ -104,22 +104,19 @@
 
     local_doc.wait()
     wide = doc_ref.shape[1]
+    per = R // wide
     number = lax.broadcasted_iota(jnp.int32, (32, wide), 0)
-    count = jnp.zeros((32, wide), jnp.int32)
-    for r in range(doc_ref.shape[0]):
-        count = count + (doc_ref[pl.ds(r, 1), :] < number).astype(jnp.int32)
-    first = jnp.sum(count, axis=1, keepdims=True)
     lane = lax.broadcasted_iota(jnp.int32, (1, wide), 1)
-    per = R // wide
+    qt[HD + 32:2 * HD, :] = jnp.zeros((HD - 32, 8 * R), jnp.bfloat16)
     for b in range(2):
         block = chip * 2 + (core if b == 0 else 1 - core)
         for t in range(per):
             row = block * per + t
             own = doc_ref[pl.ds(row, 1), :]
-            low[b:b + 1, t * wide:(t + 1) * wide] = jnp.sum(
-                jnp.where(own == number, first, 0), axis=0, keepdims=True
-            )
+            fence = jnp.where(own == number, 0.0, HIDDEN).astype(jnp.bfloat16)
             high[b:b + 1, t * wide:(t + 1) * wide] = lane + row * wide
+            for g in (2 * b, 2 * b + 1, 2 * b + 4, 2 * b + 5):
+                qt[HD:HD + 32, g * R + t * wide:g * R + (t + 1) * wide] = fence
 
     stat[0:8, :] = jnp.full((8, R), HIDDEN, jnp.float32)
     stat[8:24, :] = jnp.zeros((16, R), jnp.float32)
@@ -143,8 +140,13 @@
     to_core, to_plane, to_corner = swap(0, 0, 1, mate), swap(1, 0, 2, zmate), swap(2, 2, 3, mate)
 
     def kv_send(n, src, dst, device):
-        return remote(kv.at[src], kv.at[dst], ks_sem.at[n], kr_sem.at[dst], device)
-
+        return [
+            remote(kv.at[src, pl.ds(i * half, half)], kv.at[dst, pl.ds(i * half, half)],
+                   ks_sem.at[n, i], kr_sem.at[dst, i], device)
+            for i in range(2)
+        ]
+
+    half = R // 2
     own_sends, near_sends, next_sends = [], [], []
     for e in range(1, 3):
         own_sends.append(
@@ -161,13 +163,14 @@
         reaches = wraps | (core == 1) if e == 1 else wraps
         next_sends.append((holds & (x >= 2) & reaches, kv_send(8 + e, 4 + column, 4 + column, there)))
 
-    def start_all(sends):
-        for cond, copy in sends:
-            pl.when(cond)(copy.start)
+    def start_all(sends, i):
+        for cond, copies in sends:
+            pl.when(cond)(copies[i].start)
 
     for copy in local_kv:
         pl.when(holds)(copy.wait)
-    start_all(own_sends)
+    for i in range(2):
+        start_all(own_sends, i)
     for copy in local_q:
         copy.wait()
 
@@ -180,11 +183,16 @@
     for copy in to_core:
         copy.wait()
     for b in range(2):
-        qt[:, b * 2 * R:(b + 1) * 2 * R] = qc[b * 2 * R:(b + 1) * 2 * R, :].T
+        qt[0:HD, b * 2 * R:(b + 1) * 2 * R] = qc[b * 2 * R:(b + 1) * 2 * R, :].T
         ot[:, b * 2 * R:(b + 1) * 2 * R] = oc[b * 2 * R:(b + 1) * 2 * R, :].T
 
+    def kv_half(j, i):
+        rows = kv.at[j, pl.ds(i * half, half)]
+        remote(rows, rows, ks_sem.at[0, 0], kr_sem.at[j, i], mate).wait_recv()
+
     def kv_arrived(j):
-        remote(kv.at[j], kv.at[j], ks_sem.at[0], kr_sem.at[j], mate).wait_recv()
+        for i in range(2):
+            kv_half(j, i)
 
     def slot(j):
         a = lax.div(j, 2)
@@ -195,16 +203,32 @@
 
     row_in_block = lax.broadcasted_iota(jnp.int32, (R, R), 0)
 
+    def mark_documents(j, d):
+        for t in range(per):
+            own = doc_ref[pl.ds(((chip - d) * 2 + core) * per + t, 1), :]
+            hot = jnp.where(own == number, 1.0, 0.0)
+            hot = jnp.concatenate([hot, jnp.zeros((HD - 32, wide), jnp.float32)], axis=0)
+            marks[j, t * wide:(t + 1) * wide, :] = hot.T.astype(jnp.bfloat16)
+
     def stats_block(z, j, d):
-        key_pos = row_in_block + ((chip - d) * 2 + core) * R
-        keys = kv[j, :, 0:HD]
+        @pl.when(d == 0)
+        def _():
+            stats_groups(z, j, True)
+
+        @pl.when(d != 0)
+        def _():
+            stats_groups(z, j, False)
+
+    def stats_groups(z, j, diagonal):
+        key_pos = row_in_block + (chip * 2 + core) * R
+        keys = jnp.concatenate([kv[j, :, 0:HD], marks[j]], axis=1)
         values = kv[j, :, HD:2 * HD]
         for g in range(4 * z, 4 * z + 4):
             b = (g // 2) % 2
             sl = slice(g * R, (g + 1) * R)
             s = jnp.dot(keys, qt[:, sl], preferred_element_type=jnp.float32) * SCALE2
-            ok = (key_pos >= low[b:b + 1, :]) & (key_pos <= high[b:b + 1, :])
-            s = jnp.where(ok, s, HIDDEN)
+            if diagonal:
+                s = jnp.where(key_pos <= high[b:b + 1, :], s, HIDDEN)
             m_old = stat[g:g + 1, :]
             m_new = jnp.maximum(m_old, jnp.max(s, axis=0, keepdims=True))
             alpha = jnp.exp2(m_old - m_new)
@@ -220,13 +244,15 @@
     def stats_step(j, carry):
         @pl.when((j == 1) & (x >= 1) & jnp.logical_not(holds))
         def _():
-            kv_arrived(2 + column)
-            start_all(near_sends)
+            for i in range(2):
+                kv_half(2 + column, i)
+                start_all(near_sends, i)
 
         @pl.when((j == 2) & (x >= 2) & holds)
         def _():
-            kv_arrived(4 + column)
-            start_all(next_sends)
+            for i in range(2):
+                kv_half(4 + column, i)
+                start_all(next_sends, i)
 
         @pl.when(j == 4)
         def _():
@@ -243,6 +269,7 @@
             def _():
                 kv_arrived(j)
 
+            mark_documents(j, d)
             stats_block(0, j, d)
 
         return carry
@@ -252,7 +279,7 @@
     for copy in to_corner:
         copy.wait()
     for b in range(2, 4):
-        qt[:, b * 2 * R:(b + 1) * 2 * R] = qc[b * 2 * R:(b + 1) * 2 * R, :].T
+        qt[0:HD, b * 2 * R:(b + 1) * 2 * R] = qc[b * 2 * R:(b + 1) * 2 * R, :].T
         ot[:, b * 2 * R:(b + 1) * 2 * R] = oc[b * 2 * R:(b + 1) * 2 * R, :].T
 
     def stats_other(j, carry):
@@ -344,7 +371,6 @@
                 p = prob[j, :, sl] * factor
                 plow.append(p.astype(jnp.bfloat16))
                 slow.append((p * (dprob[j, :, sl] - norm[8 + g:9 + g, :])).astype(jnp.bfloat16))
-            keys = kv[j, :, 0:HD]
             dk = jnp.dot(jnp.concatenate(slow, axis=1), qc[...], preferred_element_type=jnp.float32)
             dv = jnp.dot(jnp.concatenate(plow, axis=1), oc[...], preferred_element_type=jnp.float32)
 
@@ -359,15 +385,28 @@
                 part[j, :, HD:2 * HD] = dv.astype(jnp.bfloat16)
                 part_copy(j).start()
 
+            for g in range(8):
+                gscore[j, :, g * R:(g + 1) * R] = slow[g]
+
+        return carry
+
+    lax.fori_loop(0, SLOTS, grads_step, 0)
+
+    def query_step(j, carry):
+        a, ky, d, valid = slot(j)
+
+        @pl.when(valid)
+        def _():
+            keys = kv[j, :, 0:HD]
             for r in range(4):
                 dqt[r] += lax.dot_general(
-                    keys, jnp.concatenate(slow[2 * r:2 * r + 2], axis=1),
+                    keys, gscore[j, :, r * 2 * R:(r + 1) * 2 * R],
                     (((0,), (0,)), ((), ())), preferred_element_type=jnp.float32,
                 )
 
         return carry
 
-    lax.fori_loop(0, SLOTS, grads_step, 0)
+    lax.fori_loop(0, SLOTS, query_step, 0)
 
     dq_swaps = [
         remote(dqt.at[2 * i + 1], dq_in.at[i], ds_sem.at[i], dr_sem.at[i], mate) for i in range(2)
@@ -435,8 +474,9 @@
     dk_out[...] = (zsum[0:wide_out, :] * SCALE).astype(jnp.bfloat16)
     dv_out[...] = zsum[wide_out:2 * wide_out, :].astype(jnp.bfloat16)
 
-    for cond, copy in own_sends + near_sends + next_sends + [(x_here[a], x_copy[a]) for a in (1, 2)]:
-        pl.when(cond)(copy.wait_send)
+    for cond, copies in own_sends + near_sends + next_sends + [(x_here[a], [x_copy[a]]) for a in (1, 2)]:
+        for copy in copies:
+            pl.when(cond)(copy.wait_send)
 
     def parts_sent(j, carry):
         a, ky, d, valid = slot(j)
@@ -475,13 +515,14 @@
         pltpu.VMEM((SLOTS, R, 2 * HD), bf),
         pltpu.VMEM((8 * R, HD), bf),
         pltpu.VMEM((8 * R, HD), bf),
+        pltpu.VMEM((2 * HD, 8 * R), bf),
         pltpu.VMEM((HD, 8 * R), bf),
-        pltpu.VMEM((HD, 8 * R), bf),
-        pltpu.VMEM((2, R), i32),
+        pltpu.VMEM((SLOTS, R, HD), bf),
         pltpu.VMEM((2, R), i32),
         pltpu.VMEM((SLOTS, R, 8 * R), f32),
         pltpu.VMEM((SLOTS, R, 8 * R), f32),
         pltpu.VMEM((SLOTS, 8, R), f32),
+        pltpu.VMEM((SLOTS, R, 8 * R), bf),
         pltpu.VMEM((24, R), f32),
         pltpu.VMEM((3, 24, R), f32),
         pltpu.VMEM((16, R), f32),
@@ -498,7 +539,7 @@
         pltpu.VMEM((share, 2 * HD // share, R), bf),
         pltpu.VMEM((share // 2, 2 * HD // share, R), bf),
         pltpu.VMEM((2 * HD // share, R), f32),
-        dma((7,)), dma((6,)), dma((6,)), dma((12,)), dma((SLOTS,)), dma((3,)), dma((3,)),
+        dma((7,)), dma((6,)), dma((6,)), dma((12, 2)), dma((SLOTS, 2)), dma((3,)), dma((3,)),
         dma((SLOTS,)), dma((4, SIDE)), dma((2,)), dma((2,)), dma((share,)), dma((share // 2,)),
         dma((3,)), dma((3,)), pltpu.SemaphoreType.REGULAR,
     ]

time: 51.8 us -> 50.7 us (0.979)
  the two profiles are of different devices: /device:TPU:8 before, /device:TPU:132 now
where the time goes in v6:
time: 50.7 us; the launch traced here: 50.5 us
  Pallas kernels  49.8 us (98%)
  between operations  0.64 us (1%)
    pallas_call x1, Pallas kernels, on_device(): pl.pallas_call(functools.partial(kernel, share), out_shape=(pltpu.VMEM((R...  49.1 us

profile of v6, /device:TPU:132, one launch (start us, length us, event | category | flops | bytes accessed | tf_op | source)
XLA Modules:
  0.0 50.5 jit_solution(11019809678094134902)
XLA Ops:
  0.6 49.1 %shard_map.76 = (bf16[256,256]{1,0:T(8,128)(2,1)S(1)}, bf16[32,256]{1,0:T(8,128)(2,1)S(1)}, bf16[32,256]{1,0:T(8,128)(2,1)S(1)}) custom-call(bf16[256,256]{1,0:T(8,128)(2,1)} %q_ref.1, bf16[256,1024]{1,0:T(8,128)(2,1)} %k_ref.1, bf16[256,1024]{1,0:T(8,128)(2,1)} %v_ref.1, bf16[256,256]{1,0:T(8,128)(2,1)} %o_ref.1, s32[64,128]{1,0:T(8,128)} %bitcast.3), custom_call_target="tpu_custom_call" | custom-call | tf_op jit(solution)/shard_map/pallas_call | solution.py:548
  49.8 0.7 %shard_map.77 = (bf16[256,256]{1,0:T(8,128)(2,1)}, bf16[32,256]{1,0:T(8,128)(2,1)}, bf16[32,256]{1,0:T(8,128)(2,1)}) custom-call(bf16[256,256]{1,0:T(8,128)(2,1)S(1)} %get-tuple-element.9.a_ref, bf16[32,256]{1,0:T(8,128)(2,1)S(1)} %get-tuple-element.10.b_ref, bf16[32,256]{1,0:T(8,128)(2,1)S(1)} %get-tuple-element.11.c_ref), custom_call_target="tpu_custom_call" | custom-call | tf_op jit(solution)/shard_map/pallas_call | solution.py:562

commit v7 on v6

--- a/solution.py
+++ b/solution.py
@@ -323,34 +323,45 @@
     def part_copy(j):
         a, ky, d, valid = slot(j)
         tx = x - 3 * lax.div(a, 3)
-        return remote(part.at[j], got.at[a, y], ps_sem.at[j], pr_sem.at[a, y], at(tx, ky))
-
-    def part_arrived(a, sy):
-        remote(got.at[a, sy], got.at[a, sy], ps_sem.at[0], pr_sem.at[a, sy], mate).wait_recv()
-
-    def gather_row(a, e, cond):
+        return [
+            remote(part.at[j, pl.ds(i * half, half)], got.at[a, y, pl.ds(i * half, half)],
+                   ps_sem.at[j, i], pr_sem.at[a, y, i], at(tx, ky))
+            for i in range(2)
+        ]
+
+    def part_arrived(a, sy, i):
+        rows = got.at[a, sy, pl.ds(i * half, half)]
+        remote(rows, rows, ps_sem.at[0, 0], pr_sem.at[a, sy, i], mate).wait_recv()
+
+    def gather_row(a, e, i, cond):
         sy = lax.rem(y + e, SIDE)
+        rows = slice(i * half, (i + 1) * half)
 
         @pl.when(cond)
         def _():
-            part_arrived(a, sy)
-            accf[a] += got[a, sy].astype(jnp.float32)
+            part_arrived(a, sy, i)
+            accf[a, rows, :] += got[a, sy, rows, :].astype(jnp.float32)
 
     def x_hand_over(a):
-        for e in range(1, SIDE):
-            wraps = y + e >= SIDE
-            reaches = True if a == 1 else (wraps | (core == 1) if e == 1 else wraps)
-            gather_row(a, e, x_here[a] & reaches)
-
-        @pl.when(x_here[a])
-        def _():
-            xout[a - 1] = accf[a].astype(jnp.bfloat16)
-            x_copy[a].start()
+        for i in range(2):
+            rows = slice(i * half, (i + 1) * half)
+            for e in range(1, SIDE):
+                wraps = y + e >= SIDE
+                reaches = True if a == 1 else (wraps | (core == 1) if e == 1 else wraps)
+                gather_row(a, e, i, x_here[a] & reaches)
+
+            @pl.when(x_here[a])
+            def _(i=i, rows=rows):
+                xout[a - 1, rows, :] = accf[a, rows, :].astype(jnp.bfloat16)
+                x_copy[a][i].start()
 
     x_here = {1: (x >= 1) & jnp.logical_not(holds), 2: (x >= 2) & holds}
     x_copy = {
-        a: remote(xout.at[a - 1], xin.at[a - 1], xs_sem.at[a - 1], xr_sem.at[a - 1],
-                  at(lax.rem(x - a + SIDE, SIDE), y))
+        a: [
+            remote(xout.at[a - 1, pl.ds(i * half, half)], xin.at[a - 1, pl.ds(i * half, half)],
+                   xs_sem.at[a - 1, i], xr_sem.at[a - 1, i], at(lax.rem(x - a + SIDE, SIDE), y))
+            for i in range(2)
+        ]
         for a in (1, 2)
     }
 
@@ -383,7 +394,8 @@
             def _():
                 part[j, :, 0:HD] = dk.astype(jnp.bfloat16)
                 part[j, :, HD:2 * HD] = dv.astype(jnp.bfloat16)
-                part_copy(j).start()
+                for copy in part_copy(j):
+                    copy.start()
 
             for g in range(8):
                 gscore[j, :, g * R:(g + 1) * R] = slow[g]
@@ -421,18 +433,22 @@
     zq_swap = remote(zq_out, zq_in, ds_sem.at[2], dr_sem.at[2], zmate)
     zq_swap.start()
 
-    for e in range(1, SIDE):
-        gather_row(0, e, holds & (y + e < SIDE))
+    for i in range(2):
+        for e in range(1, SIDE):
+            gather_row(0, e, i, holds & (y + e < SIDE))
 
     for a in (1, 2):
         @pl.when(holds & (x + a < SIDE))
         def _():
-            remote(xin.at[a - 1], xin.at[a - 1], xs_sem.at[0], xr_sem.at[a - 1], mate).wait_recv()
+            for i in range(2):
+                rows = xin.at[a - 1, pl.ds(i * half, half)]
+                remote(rows, rows, xs_sem.at[0, 0], xr_sem.at[a - 1, i], mate).wait_recv()
             accf[0] += xin[a - 1].astype(jnp.float32)
 
     @pl.when(far_out)
     def _():
-        part_arrived(3, 0)
+        part_arrived(3, 0, 0)
+        part_arrived(3, 0, 1)
         accf[0] += got[3, 0].astype(jnp.float32)
 
     wide_out = HD // share
@@ -474,7 +490,7 @@
     dk_out[...] = (zsum[0:wide_out, :] * SCALE).astype(jnp.bfloat16)
     dv_out[...] = zsum[wide_out:2 * wide_out, :].astype(jnp.bfloat16)
 
-    for cond, copies in own_sends + near_sends + next_sends + [(x_here[a], [x_copy[a]]) for a in (1, 2)]:
+    for cond, copies in own_sends + near_sends + next_sends + [(x_here[a], x_copy[a]) for a in (1, 2)]:
         for copy in copies:
             pl.when(cond)(copy.wait_send)
 
@@ -483,7 +499,8 @@
 
         @pl.when(valid & (ky != y))
         def _():
-            part_copy(j).wait_send()
+            for copy in part_copy(j):
+                copy.wait_send()
 
         return carry
 
@@ -540,7 +557,7 @@
         pltpu.VMEM((share // 2, 2 * HD // share, R), bf),
         pltpu.VMEM((2 * HD // share, R), f32),
         dma((7,)), dma((6,)), dma((6,)), dma((12, 2)), dma((SLOTS, 2)), dma((3,)), dma((3,)),
-        dma((SLOTS,)), dma((4, SIDE)), dma((2,)), dma((2,)), dma((share,)), dma((share // 2,)),
+        dma((SLOTS, 2)), dma((4, SIDE, 2)), dma((2, 2)), dma((2, 2)), dma((share,)), dma((share // 2,)),
         dma((3,)), dma((3,)), pltpu.SemaphoreType.REGULAR,
     ]
     vmem = pl.BlockSpec(memory_space=pltpu.VMEM)

time: 50.7 us -> 49.9 us (0.984)
  the two profiles are of different devices: /device:TPU:132 before, /device:TPU:8 now
where the time goes in v7:
time: 49.9 us; the launch traced here: 49.7 us
  Pallas kernels  49.1 us (98%)
  between operations  0.64 us (1%)
    pallas_call x1, Pallas kernels, on_device(): pl.pallas_call(functools.partial(kernel, share), out_shape=(pltpu.VMEM((R...  48.4 us

profile of v7, /device:TPU:8, one launch (start us, length us, event | category | flops | bytes accessed | tf_op | source)
XLA Modules:
  0.0 49.7 jit_solution(3934764164813850200)
XLA Ops:
  0.6 48.4 %shard_map.76 = (bf16[256,256]{1,0:T(8,128)(2,1)S(1)}, bf16[32,256]{1,0:T(8,128)(2,1)S(1)}, bf16[32,256]{1,0:T(8,128)(2,1)S(1)}) custom-call(bf16[256,256]{1,0:T(8,128)(2,1)} %q_ref.1, bf16[256,1024]{1,0:T(8,128)(2,1)} %k_ref.1, bf16[256,1024]{1,0:T(8,128)(2,1)} %v_ref.1, bf16[256,256]{1,0:T(8,128)(2,1)} %o_ref.1, s32[64,128]{1,0:T(8,128)} %bitcast.3), custom_call_target="tpu_custom_call" | custom-call | tf_op jit(solution)/shard_map/pallas_call | solution.py:565
  49.1 0.7 %shard_map.77 = (bf16[256,256]{1,0:T(8,128)(2,1)}, bf16[32,256]{1,0:T(8,128)(2,1)}, bf16[32,256]{1,0:T(8,128)(2,1)}) custom-call(bf16[256,256]{1,0:T(8,128)(2,1)S(1)} %get-tuple-element.9.a_ref, bf16[32,256]{1,0:T(8,128)(2,1)S(1)} %get-tuple-element.10.b_ref, bf16[32,256]{1,0:T(8,128)(2,1)S(1)} %get-tuple-element.11.c_ref), custom_call_target="tpu_custom_call" | custom-call | tf_op jit(solution)/shard_map/pallas_call | solution.py:579

commit v8 on v7

--- a/solution.py
+++ b/solution.py
@@ -256,10 +256,9 @@
 
         @pl.when(j == 4)
         def _():
-            for copy in to_plane:
-                copy.wait()
-            for copy in to_corner:
-                copy.start()
+            for came, goes in zip(to_plane, to_corner):
+                came.wait()
+                goes.start()
 
         a, ky, d, valid = slot(j)
 
@@ -433,43 +432,46 @@
     zq_swap = remote(zq_out, zq_in, ds_sem.at[2], dr_sem.at[2], zmate)
     zq_swap.start()
 
-    for i in range(2):
-        for e in range(1, SIDE):
-            gather_row(0, e, i, holds & (y + e < SIDE))
-
-    for a in (1, 2):
-        @pl.when(holds & (x + a < SIDE))
-        def _():
-            for i in range(2):
-                rows = xin.at[a - 1, pl.ds(i * half, half)]
-                remote(rows, rows, xs_sem.at[0, 0], xr_sem.at[a - 1, i], mate).wait_recv()
-            accf[0] += xin[a - 1].astype(jnp.float32)
-
-    @pl.when(far_out)
-    def _():
-        part_arrived(3, 0, 0)
-        part_arrived(3, 0, 1)
-        accf[0] += got[3, 0].astype(jnp.float32)
-
     wide_out = HD // share
     pair = lax.div(member, 2)
     z_sends = []
-    for e in range(1, share):
-        to = lax.rem(member + e, share)
-        z_sends.append(
-            remote(zout.at[to], zin.at[pair], zs_sem.at[to], zr_sem.at[pair], (grp - member + to, srv))
-        )
+    for i in range(2):
+        rows = slice(i * half, (i + 1) * half)
+        for e in range(1, SIDE):
+            gather_row(0, e, i, holds & (y + e < SIDE))
+        for a in (1, 2):
+            @pl.when(holds & (x + a < SIDE))
+            def _(a=a, i=i, rows=rows):
+                came = xin.at[a - 1, pl.ds(i * half, half)]
+                remote(came, came, xs_sem.at[0, 0], xr_sem.at[a - 1, i], mate).wait_recv()
+                accf[0, rows, :] += xin[a - 1, rows, :].astype(jnp.float32)
+
+        @pl.when(far_out)
+        def _(i=i, rows=rows):
+            part_arrived(3, 0, i)
+            accf[0, rows, :] += got[3, 0, rows, :].astype(jnp.float32)
+
+        goes = []
+        for e in range(1, share):
+            to = lax.rem(member + e, share)
+            goes.append(
+                remote(zout.at[i, to], zin.at[i, pair], zs_sem.at[to, i], zr_sem.at[pair, i], (grp - member + to, srv))
+            )
+        z_sends += goes
+
+        @pl.when(holds)
+        def _(i=i, rows=rows, goes=goes):
+            turned = accf[0, rows, :].T
+            for m in range(share):
+                for s in range(2):
+                    piece = turned[s * HD + m * wide_out:s * HD + (m + 1) * wide_out, :]
+                    zown[m, s * wide_out:(s + 1) * wide_out, rows] = piece
+                    zout[i, m, s * wide_out:(s + 1) * wide_out, :] = piece.astype(jnp.bfloat16)
+            for copy in goes:
+                copy.start()
 
     @pl.when(holds)
     def _():
-        turned = accf[0].T
-        for m in range(share):
-            for s in range(2):
-                piece = turned[s * HD + m * wide_out:s * HD + (m + 1) * wide_out, :]
-                zown[m, s * wide_out:(s + 1) * wide_out, :] = piece
-                zout[m, s * wide_out:(s + 1) * wide_out, :] = piece.astype(jnp.bfloat16)
-        for copy in z_sends:
-            copy.start()
         zsum[...] = zown[member]
 
     @pl.when(jnp.logical_not(holds))
@@ -484,8 +486,9 @@
     for w in range(share // 2):
         @pl.when(jnp.logical_not(holds & (pair == w)))
         def _():
-            remote(zin.at[w], zin.at[w], zs_sem.at[0], zr_sem.at[w], mate).wait_recv()
-            zsum[...] += zin[w].astype(jnp.float32)
+            for i in range(2):
+                remote(zin.at[i, w], zin.at[i, w], zs_sem.at[0, 0], zr_sem.at[w, i], mate).wait_recv()
+                zsum[:, i * half:(i + 1) * half] += zin[i, w].astype(jnp.float32)
 
     dk_out[...] = (zsum[0:wide_out, :] * SCALE).astype(jnp.bfloat16)
     dv_out[...] = zsum[wide_out:2 * wide_out, :].astype(jnp.bfloat16)
@@ -553,11 +556,11 @@
         pltpu.VMEM((2, R, 2 * HD), bf),
         pltpu.VMEM((2, R, 2 * HD), bf),
         pltpu.VMEM((share, 2 * HD // share, R), f32),
-        pltpu.VMEM((share, 2 * HD // share, R), bf),
-        pltpu.VMEM((share // 2, 2 * HD // share, R), bf),
+        pltpu.VMEM((2, share, 2 * HD // share, R // 2), bf),
+        pltpu.VMEM((2, share // 2, 2 * HD // share, R // 2), bf),
         pltpu.VMEM((2 * HD // share, R), f32),
         dma((7,)), dma((6,)), dma((6,)), dma((12, 2)), dma((SLOTS, 2)), dma((3,)), dma((3,)),
-        dma((SLOTS, 2)), dma((4, SIDE, 2)), dma((2, 2)), dma((2, 2)), dma((share,)), dma((share // 2,)),
+        dma((SLOTS, 2)), dma((4, SIDE, 2)), dma((2, 2)), dma((2, 2)), dma((share, 2)), dma((share // 2, 2)),
         dma((3,)), dma((3,)), pltpu.SemaphoreType.REGULAR,
     ]
     vmem = pl.BlockSpec(memory_space=pltpu.VMEM)

time: 49.9 us -> 50.5 us (1.012)
  the two profiles are of different devices: /device:TPU:8 before, /device:TPU:284 now
where the time goes in v8:
time: 50.5 us; the launch traced here: 50.3 us
  Pallas kernels  49.7 us (98%)
  between operations  0.64 us (1%)
    pallas_call x1, Pallas kernels, on_device(): pl.pallas_call(functools.partial(kernel, share), out_shape=(pltpu.VMEM((R...  49 us

profile of v8, /device:TPU:284, one launch (start us, length us, event | category | flops | bytes accessed | tf_op | source)
XLA Modules:
  0.0 50.3 jit_solution(531675672887533797)
XLA Ops:
  0.6 49.0 %shard_map.76 = (bf16[256,256]{1,0:T(8,128)(2,1)S(1)}, bf16[32,256]{1,0:T(8,128)(2,1)S(1)}, bf16[32,256]{1,0:T(8,128)(2,1)S(1)}) custom-call(bf16[256,256]{1,0:T(8,128)(2,1)} %q_ref.1, bf16[256,1024]{1,0:T(8,128)(2,1)} %k_ref.1, bf16[256,1024]{1,0:T(8,128)(2,1)} %v_ref.1, bf16[256,256]{1,0:T(8,128)(2,1)} %o_ref.1, s32[64,128]{1,0:T(8,128)} %bitcast.3), custom_call_target="tpu_custom_call" | custom-call | tf_op jit(solution)/shard_map/pallas_call | solution.py:568
  49.6 0.7 %shard_map.77 = (bf16[256,256]{1,0:T(8,128)(2,1)}, bf16[32,256]{1,0:T(8,128)(2,1)}, bf16[32,256]{1,0:T(8,128)(2,1)}) custom-call(bf16[256,256]{1,0:T(8,128)(2,1)S(1)} %get-tuple-element.9.a_ref, bf16[32,256]{1,0:T(8,128)(2,1)S(1)} %get-tuple-element.10.b_ref, bf16[32,256]{1,0:T(8,128)(2,1)S(1)} %get-tuple-element.11.c_ref), custom_call_target="tpu_custom_call" | custom-call | tf_op jit(solution)/shard_map/pallas_call | solution.py:582
